TPU v7x, 256 devices: a whole 4x4x8 slice. The times are simulated.
256 devices in a mesh: member: 16 (over x, y_hi, core), tile: 16 (over z, y_lo).
Axes of the slice: x: 4, y: 4 (y_hi: 2, y_lo: 2; y = y_hi * 2 + y_lo), z: 8, core: 2. Of those that a mesh axis runs over, the one named last changes fastest.
Arguments:
- control: float32 [256, 16, 4, 4096], P('member', 'tile'), may hold values from -6 to 6
- perturbations: float32 [256, 16, 4, 4, 4096], P('member', 'tile'), may hold values from -1.5 to 1.5
- diffusivity: float32 [16, 4096], P('tile'), may hold values from 0.02 to 0.24
- flow: float32 [2, 16, 4, 4], P(None, 'tile'), may hold values from 0.02 to 0.22
- observed: float32 [16, 4, 4, 4096], P('tile'), may hold values from -6 to 6
- obs_weight: float32 [16, 4, 4, 4096], P('tile'), may hold values from 0.3 to 3
- neighbour_tile: int32 [16, 4], replicated, may hold values from 0 to 15, as said below
- neighbour_edge: int32 [16, 4], replicated, may hold values from 0 to 3
- departure: int32 [16, 4, 64], replicated, may hold values from 0 to 63, as said below
Outputs:
- gradient: float32 [256, 16, 4, 4096], P('member', 'tile')
Inputs may be any that keep to these rules, and one draw needn't show every extreme that they name: `neighbour_tile`: edges are glued in pairs: if edge e of tile t meets edge e2 of tile u, then edge e2 of tile u meets edge e of tile t. `departure`: each row is 0 to 63 in order or reversed, the same way for both edges of a glued pair.
All inputs are finite; a program needn't handle non-finite values.
Results may differ from a plain program's by a relative error of at most 0.0001.
Values sent between devices are 32-bit elements; how exact they have to be, the bound alone decides.
No kernel may reach another device: no remote copies, remote signals or barrier semaphores. Data moves between devices by JAX's collectives and lax.ppermute only.
A program may use at most 128 MiB of HBM per device.

v0:
```python
import jax
import jax.numpy as jnp
from jax import lax
from jax.sharding import PartitionSpec as P

S = 64
V = 4
L = 4
SWEEPS = 8
STEPS = 2


PRECISE = lax.Precision.HIGHEST


def joined_along(pieces, dim):
    dims = list(pieces.shape[1:])
    dims[dim] *= pieces.shape[0]
    return jnp.moveaxis(pieces, 0, dim).reshape(dims)


def sent_to_all(shard, axis):
    copies = jnp.broadcast_to(shard, (lax.axis_size(axis), *shard.shape))
    return lax.all_to_all(copies, axis, split_axis=0, concat_axis=0, tiled=True)


def gathered_copies(shard, axis, dim):
    return joined_along(sent_to_all(shard, axis), dim)


def cut_along(shard, dim, length):
    before, after = (shard.shape[:dim], shard.shape[dim + 1 :])
    return jnp.moveaxis(shard.reshape(*before, length, -1, *after), dim, 0)


def sum_at_owner(shard, axis, dim):
    length = lax.axis_size(axis)
    pieces = lax.all_to_all(cut_along(shard, dim, length), axis, 0, 0, tiled=True)
    return jnp.sum(pieces, axis=0)


def flat_strips(values):
    return jnp.stack(
        [values[..., :S], values[..., -S:], values[..., ::S], values[..., S - 1 :: S]], axis=2
    )


def reverse_where(flags, strips):
    return jnp.where(flags[None, :, :, None, None], strips[..., ::-1], strips)


def table_rows(neighbour_tile, neighbour_edge, departure, first, row_count):
    own_tile = lax.dynamic_slice_in_dim(neighbour_tile, first, row_count, 0)
    own_edge = lax.dynamic_slice_in_dim(neighbour_edge, first, row_count, 0)
    own_departure = lax.dynamic_slice_in_dim(departure, first, row_count, 0)
    source = (own_tile * 4 + own_edge).reshape(-1)
    flags = own_departure[:, :, 0] != 0
    return (source, flags)


def fetch(strips, collect, source):
    pcount, tcount, qcount = (strips.shape[0], strips.shape[1], strips.shape[3])
    everyone = collect(strips.reshape(pcount, tcount, 4, qcount * S))
    everyone = everyone.reshape(pcount, everyone.shape[1] * 4, qcount, S)
    return jnp.take(everyone, source, axis=1).reshape(pcount, tcount, 4, qcount, S)


def forward_step(values, factors, collect, tables):
    source, flags = tables
    cell_count = values.shape[-1]
    column = jnp.arange(cell_count, dtype=jnp.int32) % S
    ghosts = reverse_where(flags, fetch(flat_strips(values), collect, source))
    zero_one = jnp.zeros(values.shape[:-1] + (1,), jnp.float32)
    before_rows = jnp.concatenate([ghosts[:, :, 0], values[..., :-S]], axis=-1)
    after_rows = jnp.concatenate([values[..., S:], ghosts[:, :, 1]], axis=-1)
    before_cols = jnp.where(
        column == 0,
        jnp.repeat(ghosts[:, :, 2], S, axis=-1),
        jnp.concatenate([zero_one, values[..., :-1]], axis=-1),
    )
    after_cols = jnp.where(
        column == S - 1,
        jnp.repeat(ghosts[:, :, 3], S, axis=-1),
        jnp.concatenate([values[..., 1:], zero_one], axis=-1),
    )
    return (
        factors[0] * values
        + factors[1] * before_rows
        + factors[2] * after_rows
        + factors[3] * before_cols
        + factors[4] * after_cols
    )


def adjoint_step(values, factors, collect, tables):
    source, flags = tables
    cell_count = values.shape[-1]
    column = jnp.arange(cell_count, dtype=jnp.int32) % S
    parts = [factors[1 + which] * values for which in range(4)]
    zero_one = jnp.zeros(values.shape[:-1] + (1,), jnp.float32)
    zero_row = jnp.zeros(values.shape[:-1] + (S,), jnp.float32)
    zero_rest = jnp.zeros(values.shape[:-1] + (cell_count - S,), jnp.float32)
    inner = factors[0] * values
    inner = inner + jnp.concatenate([parts[0][..., S:], zero_row], axis=-1)
    inner = inner + jnp.concatenate([zero_row, parts[1][..., :-S]], axis=-1)
    inner = inner + jnp.where(
        column == S - 1, 0.0, jnp.concatenate([parts[2][..., 1:], zero_one], axis=-1)
    )
    inner = inner + jnp.where(
        column == 0, 0.0, jnp.concatenate([zero_one, parts[3][..., :-1]], axis=-1)
    )
    outward = jnp.stack(
        [parts[0][..., :S], parts[1][..., -S:], parts[2][..., ::S], parts[3][..., S - 1 :: S]],
        axis=2,
    )
    incoming = fetch(reverse_where(flags, outward), collect, source)
    inner = inner + jnp.concatenate([incoming[:, :, 0], zero_rest], axis=-1)
    inner = inner + jnp.concatenate([zero_rest, incoming[:, :, 1]], axis=-1)
    inner = inner + jnp.where(column == 0, jnp.repeat(incoming[:, :, 2], S, axis=-1), 0.0)
    inner = inner + jnp.where(column == S - 1, jnp.repeat(incoming[:, :, 3], S, axis=-1), 0.0)
    return inner


def diffuse(values, diffus, tables, collect, adjoint):
    tcount = values.shape[1]
    rate = diffus.reshape(1, tcount, 1, diffus.shape[-1])
    factors = (1.0 - 4.0 * rate, rate, rate, rate, rate)
    grid = values
    for repeat in range(SWEEPS):
        if adjoint:
            grid = adjoint_step(grid, factors, collect, tables)
        else:
            grid = forward_step(grid, factors, collect, tables)
    return grid


def keep_all(strips):
    return strips


def body(
    control,
    perturbations,
    diffusivity,
    flow,
    observed,
    obs_weight,
    neighbour_tile,
    neighbour_edge,
    departure,
):
    here = lax.axis_index("tile")
    own_tables = table_rows(neighbour_tile, neighbour_edge, departure, here, 1)
    whole_tables = table_rows(neighbour_tile, neighbour_edge, departure, 0, lax.axis_size("tile"))
    whole_rate = gathered_copies(diffusivity, "tile", 0)

    def localise(values, adjoint):
        mixed = diffuse(
            lax.all_to_all(values, "tile", split_axis=0, concat_axis=1, tiled=True),
            whole_rate,
            whole_tables,
            keep_all,
            adjoint,
        )
        return lax.all_to_all(mixed, "tile", split_axis=1, concat_axis=0, tiled=True)

    smoothed = localise(control, False)
    partial_value = jnp.sum(perturbations * smoothed[:, :, None], axis=0)
    field_rows = V * L
    cell_count = control.shape[-1]
    shared = sum_at_owner(partial_value.reshape(1, field_rows, cell_count), "member", 1)
    row_count = shared.shape[1]
    first_row = lax.axis_index("member") * row_count
    states = shared.reshape(1, 1, row_count, cell_count)
    levels = (first_row + jnp.arange(row_count, dtype=jnp.int32)) % L
    target = lax.dynamic_slice_in_dim(
        observed.reshape(1, field_rows, cell_count), first_row, row_count, 1
    ).reshape(1, 1, row_count, cell_count)
    weights_here = lax.dynamic_slice_in_dim(
        obs_weight.reshape(1, field_rows, cell_count), first_row, row_count, 1
    ).reshape(1, 1, row_count, cell_count)
    level_pick = (levels[:, None] == jnp.arange(L, dtype=jnp.int32)[None, :]).astype(jnp.float32)

    def flow_factors(section):
        speeds = jnp.dot(level_pick, flow[section, 0], precision=PRECISE)
        total = jnp.sum(speeds, axis=1)
        return (
            1.0 - total[None, None, :, None],
            speeds[None, None, :, 0, None],
            speeds[None, None, :, 1, None],
            speeds[None, None, :, 2, None],
            speeds[None, None, :, 3, None],
        )

    def flow_out(strips):
        return gathered_copies(strips, "tile", 1)

    def flow_back(strips):
        return gathered_copies(strips, "tile", 1)

    for section in range(STEPS):
        states = forward_step(states, flow_factors(section), flow_out, own_tables)
    misfit = weights_here * (states - target)
    for section in reversed(range(STEPS)):
        misfit = adjoint_step(misfit, flow_factors(section), flow_back, own_tables)
    sensitivity = gathered_copies(misfit.reshape(1, row_count, cell_count), "member", 1).reshape(
        1, V, L, cell_count
    )
    projected = jnp.sum(perturbations * sensitivity[None], axis=2)
    return control + localise(projected, True)


def solution(mesh):
    in_specs = (
        P("member", "tile", None, None),
        P("member", "tile", None, None, None),
        P("tile", None),
        P(None, "tile", None, None),
        P("tile", None, None, None),
        P("tile", None, None, None),
        P(),
        P(),
        P(),
    )
    out_specs = P("member", "tile", None, None)
    return jax.shard_map(body, mesh=mesh, in_specs=in_specs, out_specs=out_specs, check_vma=False)
```

profile of v0, /device:TPU:2, one launch (start us, length us, event | category | flops | bytes accessed | tf_op | source)
XLA Modules:
  0.0 541.5 jit_solution(12913637462247298375)
XLA Ops:
  1.0 21.4 %all_to_all.80 = f32[16,1,4096]{2,1,0:T(1,128)S(1)} all-to-all(f32[16,1,4096]{2,1,0:T(1,128)S(1)} %broadcast_in_dim.543), channel_id=1, replica_groups=mesh['member'=16,'tile'=16] {'tile'}, dimensions={0} | all-to-all | bytes 524288 | tf_op jit(solution)/shard_map/all_to_all | solution.py:24
  22.3 3.7 all-to-all-start.1
  26.8 26.5 %all-to-all-done.1 = f32[16,1,4,4096]{3,2,1,0:T(4,128)S(1)} async-done(((f32[16,1,4,4096]{3,2,1,0:T(4,128)}), f32[16,1,4,4096]{3,2,1,0:T(4,128)S(1)}, u32[]{:S(2)}, u32[]{:S(2)}) %all-to-all-start.1) | async-done | bytes 1048608 | tf_op jit(solution)/shard_map/all_to_all | solution.py:159
  61.9 2.9 broadcast_in_dim.547
  66.8 2.9 broadcast_in_dim.550
  69.7 3.8 fusion.3
  81.4 2.9 broadcast_in_dim.552
  86.2 3.1 broadcast_in_dim.554
  89.3 3.5 fusion.7
  100.6 2.9 broadcast_in_dim.556
  105.4 2.9 broadcast_in_dim.558
  108.4 3.5 fusion.11
  124.5 3.3 broadcast_in_dim.562
  127.8 3.5 fusion.15
  143.9 2.9 broadcast_in_dim.566
  146.8 3.5 fusion.19
  162.9 3.1 broadcast_in_dim.570
  166.0 3.5 fusion.23
  182.1 2.9 broadcast_in_dim.574
  185.0 3.5 fusion.27
  203.3 3.1 fusion.31
  208.1 4.1 all-to-all-start.2
  215.4 23.4 %all-to-all-done.2 = f32[1,16,4,4096]{3,2,0,1:T(4,128)S(1)} async-done(((f32[1,16,4,4096]{3,2,0,1:T(4,128)}), f32[1,16,4,4096]{3,2,0,1:T(4,128)S(1)}, u32[]{:S(2)}, u32[]{:S(2)}) %all-to-all-start.2) | async-done | bytes 1048608 | tf_op jit(solution)/shard_map/all_to_all | solution.py:165
  238.8 3.5 multiply_reduce_fusion.1
  243.4 7.2 %all-to-all-start.3 = ((f32[16,1,1,4096]{3,2,1,0:T(1,128)}), f32[16,1,1,4096]{3,2,1,0:T(1,128)S(1)}, u32[]{:S(2)}, u32[]{:S(2)}) async-start(f32[16,1,1,4096]{3,2,1,0:T(1,128)} %transpose_reshape_reshape.3), calls=%async_computation.3 | async-start | bytes 524288 | tf_op jit(solution)/shard_map/all_to_all | solution.py:38
  252.1 5.5 %all-to-all-done.3 = f32[16,1,1,4096]{3,2,1,0:T(1,128)S(1)} async-done(((f32[16,1,1,4096]{3,2,1,0:T(1,128)}), f32[16,1,1,4096]{3,2,1,0:T(1,128)S(1)}, u32[]{:S(2)}, u32[]{:S(2)}) %all-to-all-start.3) | async-done | bytes 262176 | tf_op jit(solution)/shard_map/all_to_all | solution.py:38
  258.9 3.5 all-to-all-start.4
  262.6 8.5 %all-to-all-done.4 = f32[16,1,256]{2,1,0:T(1,128)S(1)} async-done(((f32[16,1,256]{2,1,0:T(1,128)}), f32[16,1,256]{2,1,0:T(1,128)S(1)}, u32[]{:S(2)}, u32[]{:S(2)}) %all-to-all-start.4) | async-done | bytes 16416 | tf_op jit(solution)/shard_map/all_to_all | solution.py:24
  277.5 3.5 all-to-all-start.5
  281.1 8.4 %all-to-all-done.5 = f32[16,1,256]{2,1,0:T(1,128)S(1)} async-done(((f32[16,1,256]{2,1,0:T(1,128)}), f32[16,1,256]{2,1,0:T(1,128)S(1)}, u32[]{:S(2)}, u32[]{:S(2)}) %all-to-all-start.5) | async-done | bytes 16416 | tf_op jit(solution)/shard_map/all_to_all | solution.py:24
  297.1 3.5 all-to-all-start.6
  300.8 8.3 %all-to-all-done.6 = f32[16,1,256]{2,1,0:T(1,128)S(1)} async-done(((f32[16,1,256]{2,1,0:T(1,128)}), f32[16,1,256]{2,1,0:T(1,128)S(1)}, u32[]{:S(2)}, u32[]{:S(2)}) %all-to-all-start.6) | async-done | bytes 16416 | tf_op jit(solution)/shard_map/all_to_all | solution.py:24
  314.9 3.5 all-to-all-start.7
  318.6 8.3 %all-to-all-done.7 = f32[16,1,256]{2,1,0:T(1,128)S(1)} async-done(((f32[16,1,256]{2,1,0:T(1,128)}), f32[16,1,256]{2,1,0:T(1,128)S(1)}, u32[]{:S(2)}, u32[]{:S(2)}) %all-to-all-start.7) | async-done | bytes 16416 | tf_op jit(solution)/shard_map/all_to_all | solution.py:24
  328.9 11.7 %all_to_all.81 = f32[16,1,1,4096]{3,2,1,0:T(1,128)S(1)} all-to-all(f32[16,1,1,4096]{3,2,1,0:T(1,128)S(1)} %broadcast_in_dim.601), channel_id=1, replica_groups=mesh['member'=16,'tile'=16] {'member'}, dimensions={0} | all-to-all | bytes 524288 | tf_op jit(solution)/shard_map/all_to_all | solution.py:24
  341.4 3.7 multiply_reduce_fusion
  345.0 32.8 %all_to_all.82 = f32[16,1,4,4096]{3,2,1,0:T(4,128)S(1)} all-to-all(f32[16,1,4,4096]{3,2,1,0:T(4,128)S(1)} %bitcast.693), channel_id=1, replica_groups=mesh['member'=16,'tile'=16] {'tile'}, dimensions={0} | all-to-all | bytes 2097152 | tf_op jit(solution)/shard_map/all_to_all | solution.py:159
  386.4 2.9 broadcast_in_dim.604
  391.3 3.0 broadcast_in_dim.606
  394.3 4.9 broadcast_multiply_fusion.3
  409.8 4.8 broadcast_multiply_fusion.1
  425.2 4.8 broadcast_multiply_fusion.5
  440.8 4.8 broadcast_multiply_fusion
  456.1 4.8 broadcast_multiply_fusion.2
  471.9 4.8 broadcast_multiply_fusion.4
  487.3 4.8 broadcast_multiply_fusion.6
  503.1 3.7 select_add_fusion
  507.5 31.0 %all_to_all.83 = f32[1,16,4,4096]{3,2,0,1:T(4,128)S(1)} all-to-all(f32[1,16,4,4096]{3,2,0,1:T(4,128)S(1)} %copy.428), channel_id=1, replica_groups=mesh['member'=16,'tile'=16] {'tile'}, dimensions={1} | all-to-all | bytes 2097152 | tf_op jit(solution)/shard_map/all_to_all | solution.py:165
  (423 shorter events, 215.4 us)
Async XLA Ops:
  0.0 26.0 %copy-start.8 = (s32[16,4]{0,1:T(4,128)S(1)}, s32[16,4]{0,1:T(4,128)}, u32[]{:S(2)}) copy-start(s32[16,4]{0,1:T(4,128)} %param.19) | copy-start | bytes 772
  0.0 26.0 %copy-start.7 = (s32[16,4]{0,1:T(4,128)S(1)}, s32[16,4]{0,1:T(4,128)}, u32[]{:S(2)}) copy-start(s32[16,4]{0,1:T(4,128)} %param.20) | copy-start | bytes 772
  0.0 26.2 %copy-start.5 = (s32[16,4,64]{2,1,0:T(4,128)S(1)}, s32[16,4,64]{2,1,0:T(4,128)}, u32[]{:S(2)}) copy-start(s32[16,4,64]{2,1,0:T(4,128)} %param.21) | copy-start | bytes 49156
  22.3 31.0 %all-to-all-start.1 = ((f32[16,1,4,4096]{3,2,1,0:T(4,128)}), f32[16,1,4,4096]{3,2,1,0:T(4,128)S(1)}, u32[]{:S(2)}, u32[]{:S(2)}) async-start(f32[16,1,4,4096]{3,2,1,0:T(4,128)} %param.13), calls=%async_computation.1 | async-start | bytes 2097152 | tf_op jit(solution)/shard_map/all_to_all | solution.py:159
  26.4 357.1 %copy-start.6 = (s32[1024]{0:T(1024)}, s32[1024]{0:T(1024)S(1)}, u32[]{:S(2)}) copy-start(s32[1024]{0:T(1024)S(1)} %pad_clamp_fusion.1) | copy-start | bytes 12292
  26.8 367.5 %copy-start = (f32[16,4096]{1,0:T(8,128)}, f32[16,4096]{1,0:T(8,128)S(1)}, u32[]{:S(2)}) copy-start(f32[16,4096]{1,0:T(8,128)S(1)} %multiply_subtract_fusion) | copy-start | bytes 786436
  206.4 6.1 %copy-start.9 = (f32[2,1,4,4]{3,2,1,0:T(4,128)S(1)}, f32[2,1,4,4]{3,2,1,0:T(4,128)}, u32[]{:S(2)}) copy-start(f32[2,1,4,4]{3,2,1,0:T(4,128)} %param.16) | copy-start | bytes 388
  208.1 30.7 %all-to-all-start.2 = ((f32[1,16,4,4096]{3,2,0,1:T(4,128)}), f32[1,16,4,4096]{3,2,0,1:T(4,128)S(1)}, u32[]{:S(2)}, u32[]{:S(2)}) async-start(f32[1,16,4,4096]{3,2,0,1:T(4,128)} %copy.368), calls=%async_computation.2 | async-start | bytes 2097152 | tf_op jit(solution)/shard_map/all_to_all | solution.py:165
  238.8 13.0 %copy-start.3 = (f32[1,4,4,4096]{3,2,1,0:T(4,128)S(1)}, f32[1,4,4,4096]{3,2,1,0:T(4,128)}, u32[]{:S(2)}) copy-start(f32[1,4,4,4096]{3,2,1,0:T(4,128)} %param.18) | copy-start | bytes 786436
  238.8 13.1 %copy-start.4 = (f32[1,4,4,4096]{3,2,1,0:T(4,128)S(1)}, f32[1,4,4,4096]{3,2,1,0:T(4,128)}, u32[]{:S(2)}) copy-start(f32[1,4,4,4096]{3,2,1,0:T(4,128)} %param.17) | copy-start | bytes 786436
  243.4 14.2 %all-to-all-start.3 = ((f32[16,1,1,4096]{3,2,1,0:T(1,128)}), f32[16,1,1,4096]{3,2,1,0:T(1,128)S(1)}, u32[]{:S(2)}, u32[]{:S(2)}) async-start(f32[16,1,1,4096]{3,2,1,0:T(1,128)} %transpose_reshape_reshape.3), calls=%async_computation.3 | async-start | bytes 524288 | tf_op jit(solution)/shard_map/all_to_all | solution.py:38
  258.9 12.2 %all-to-all-start.4 = ((f32[16,1,256]{2,1,0:T(1,128)}), f32[16,1,256]{2,1,0:T(1,128)S(1)}, u32[]{:S(2)}, u32[]{:S(2)}) async-start(f32[16,1,256]{2,1,0:T(1,128)} %reshape.3035), calls=%async_computation.4 | async-start | bytes 32768 | tf_op jit(solution)/shard_map/all_to_all | solution.py:24
  277.5 12.0 %all-to-all-start.5 = ((f32[16,1,256]{2,1,0:T(1,128)}), f32[16,1,256]{2,1,0:T(1,128)S(1)}, u32[]{:S(2)}, u32[]{:S(2)}) async-start(f32[16,1,256]{2,1,0:T(1,128)} %reshape.3037), calls=%async_computation.5 | async-start | bytes 32768 | tf_op jit(solution)/shard_map/all_to_all | solution.py:24
  297.1 12.0 %all-to-all-start.6 = ((f32[16,1,256]{2,1,0:T(1,128)}), f32[16,1,256]{2,1,0:T(1,128)S(1)}, u32[]{:S(2)}, u32[]{:S(2)}) async-start(f32[16,1,256]{2,1,0:T(1,128)} %reshape.3039), calls=%async_computation.6 | async-start | bytes 32768 | tf_op jit(solution)/shard_map/all_to_all | solution.py:24
  314.9 12.0 %all-to-all-start.7 = ((f32[16,1,256]{2,1,0:T(1,128)}), f32[16,1,256]{2,1,0:T(1,128)S(1)}, u32[]{:S(2)}, u32[]{:S(2)}) async-start(f32[16,1,256]{2,1,0:T(1,128)} %reshape.3041), calls=%async_computation.7 | async-start | bytes 32768 | tf_op jit(solution)/shard_map/all_to_all | solution.py:24
  501.4 1.7 copy-start.1
  506.8 31.7 %copy-start.2 = (f32[16,1,4,4096]{3,2,1,0:T(4,128)S(1)}, f32[16,1,4,4096]{3,2,1,0:T(4,128)}, u32[]{:S(2)}) copy-start(f32[16,1,4,4096]{3,2,1,0:T(4,128)} %param.13) | copy-start | bytes 3145732
where the time goes:
time: 552 us; the launch traced here: 541 us
  local copies, waits for them, and re-layouts  229 us (41%)
  blocking collectives  96.9 us (18%)
  other arithmetic  92.6 us (17%)
  waiting for transfers between devices  88.9 us (16%)
  starting transfers between devices  28.9 us (5%)
    mul x12, other arithmetic, adjoint_step(): parts = [factors[1 + which] * values for which in range(4)]  41.3 us
    broadcast_in_dim x20, local copies, waits for them, and re-layouts, forward_step(): jnp.repeat(ghosts[:, :, 3], S, axis=-1)  39.8 us
    broadcast_in_dim x20, local copies, waits for them, and re-layouts, forward_step(): jnp.repeat(ghosts[:, :, 2], S, axis=-1)  38.3 us
    all_to_all x4, waiting for transfers between devices, sent_to_all(): return lax.all_to_all(copies, axis, split_axis=0, concat_axis=0, tiled=True)  33.5 us
    all_to_all x2, blocking collectives, sent_to_all(): return lax.all_to_all(copies, axis, split_axis=0, concat_axis=0, tiled=True)  33.1 us
    all_to_all x1, blocking collectives, localise(): lax.all_to_all(values, 'tile', split_axis=0, concat_axis=1, tiled=True)  32.8 us
    all_to_all x1, blocking collectives, localise(): lax.all_to_all(mixed, 'tile', split_axis=1, concat_axis=0, tiled=True)  31 us
    add x9, other arithmetic, forward_step(): factors[0] * values + factors[1] * before_rows + factors[2] * after_rows  30.5 us
  transfers between devices with their start and end apart: 7, of which 7 were waited for; matrix products, arithmetic and copies ran while one was open for 1% of the time, Pallas kernels for 0%

commit v1 on v0

v1 whole, which is shorter than its diff:
```python
import functools

import jax
import jax.numpy as jnp
from jax import lax
from jax.experimental import pallas as pl
from jax.experimental.pallas import tpu as pltpu
from jax.sharding import PartitionSpec as P

S = 64
V = 4
L = 4
SWEEPS = 8
STEPS = 2
TILES = 16
PAIRS = TILES // 2
ROWS = 32
FIELD = L * ROWS
EXTRA = 3 * ROWS + 8
f32 = jnp.float32


def iota(axis):
    return lax.broadcasted_iota(jnp.int32, (8, 128), axis)


def turn(x, shift):
    shift %= 128
    return pltpu.roll(x, shift, 1) if shift else x


def swap(x):
    return pltpu.roll(x, 4, 0)


def pick(x, index):
    return jnp.take_along_axis(x, index, axis=1, mode="promise_in_bounds")


def split_halves(cells):
    low = iota(1) < S
    out = []
    for c in range(ROWS // 2):
        first, second = cells[c], cells[c + ROWS // 2]
        out.append(jnp.where(low, first, turn(second, S)))
        out.append(jnp.where(low, turn(first, S), second))
    return out


def join_halves(rows):
    low = iota(1) < S
    out = [None] * ROWS
    for c in range(ROWS // 2):
        even, odd = rows[2 * c], rows[2 * c + 1]
        out[c] = jnp.where(low, even, turn(odd, S))
        out[c + ROWS // 2] = jnp.where(low, turn(even, S), odd)
    return out


def edge_mask():
    column = iota(1) % S
    return (column == 0) | (column == S - 1)


def column_sum(values):
    mask = edge_mask()
    parts = [turn(jnp.where(mask, values[r], 0.0), 2 * r) for r in range(ROWS)]
    while len(parts) > 1:
        parts = [a + b for a, b in zip(parts[0::2], parts[1::2])]
    return parts[0]


def strips_of(top, bottom, columns):
    lane = iota(1)
    place = jnp.where(lane < S, lane, 127 - lane)
    return (
        pick(top, place),
        pick(bottom, place + S),
        pick(columns, 2 * place),
        pick(columns, (2 * place + 63) % 128),
    )


def placed_ghosts(ghosts, flips):
    lane = iota(1)
    even = lane % 2 == 0
    along = lane % S
    top = pick(ghosts[0], along + flips[0])
    bottom = pick(ghosts[1], along + flips[1])
    left = pick(ghosts[2], lane // 2 + flips[2])
    right = pick(ghosts[3], ((lane + 65) % 128) // 2 + flips[3])
    return top, bottom, jnp.where(even, left, right)


def smooth_kernel(adjoint, src_ref, flag_ref, x_ref, *refs):
    if adjoint:
        rate_ref, out_ref, state_ref, field_ref, strip_ref = refs
    else:
        out_ref, rate_ref, target_ref, speed_ref, field_ref, strip_ref = refs
    lower = iota(0) < 4
    low = iota(1) < S
    column = iota(1) % S

    def save_strips(slot, pair, top, bottom, columns):
        for edge, strip in enumerate(strips_of(top, bottom, columns)):
            strip_ref[slot, edge * TILES + 2 * pair] = strip
            strip_ref[slot, edge * TILES + 2 * pair + 1] = swap(strip)

    def load(pair, carry):
        cells = [None] * ROWS
        for k in range(ROWS // 2):
            a = x_ref[2 * pair, pl.ds(8 * k, 8), :]
            b = x_ref[2 * pair + 1, pl.ds(8 * k, 8), :]
            cells[2 * k] = jnp.where(lower, a, swap(b))
            cells[2 * k + 1] = jnp.where(lower, swap(a), b)
        values = split_halves(cells)
        if not adjoint:
            rates = []
            for c in range(ROWS):
                a = x_ref[2 * pair, pl.ds(FIELD + c, 1), :]
                b = x_ref[2 * pair + 1, pl.ds(FIELD + c, 1), :]
                rates.append(
                    jnp.where(lower, jnp.broadcast_to(a, (8, 128)), jnp.broadcast_to(b, (8, 128)))
                )
            rates = split_halves(rates)
            for r in range(ROWS):
                rate_ref[pair, r] = rates[r]
        if adjoint:
            for r in range(ROWS):
                state_ref[pair, r] = values[r]
            values = [values[r] * rate_ref[pair, r] for r in range(ROWS)]
        for r in range(ROWS):
            field_ref[pair, r] = values[r]
        save_strips(0, pair, values[0], values[ROWS - 1], column_sum(values))
        return carry

    lax.fori_loop(0, PAIRS, load, 0)

    def sweep(repeat, carry):
        slot = repeat % 2

        def one(pair, carry):
            ghosts, flips = [], []
            for d in range(4):
                first = strip_ref[slot, src_ref[8 * pair + d]]
                second = strip_ref[slot, src_ref[8 * pair + 4 + d] ^ 1]
                ghosts.append(jnp.where(lower, first, second))
                flips.append(jnp.where(lower, flag_ref[8 * pair + d], flag_ref[8 * pair + 4 + d]))
            top, bottom, sides = placed_ghosts(ghosts, flips)
            first = field_ref[pair, 0]
            last = field_ref[pair, ROWS - 1]
            before = jnp.where(low, top, turn(last, S))
            wrapped = jnp.where(low, turn(first, S), bottom)
            here = first
            mask = edge_mask()
            columns = None
            new_first = new_last = None
            for r in range(ROWS):
                after = field_ref[pair, r + 1] if r < ROWS - 1 else wrapped
                side = turn(sides, -2 * r)
                left = jnp.where(column == 0, side, turn(here, 1))
                right = jnp.where(column == S - 1, side, turn(here, -1))
                change = (before + after) + (left + right) - 4.0 * here
                if adjoint:
                    state = state_ref[pair, r] + change
                    state_ref[pair, r] = state
                    new = state * rate_ref[pair, r]
                else:
                    new = here + rate_ref[pair, r] * change
                field_ref[pair, r] = new
                edge = turn(jnp.where(mask, new, 0.0), 2 * r)
                columns = edge if columns is None else columns + edge
                if r == 0:
                    new_first = new
                new_last = new
                before, here = here, after
            save_strips(1 - slot, pair, new_first, new_last, columns)
            return carry

        lax.fori_loop(0, PAIRS, one, 0)
        return carry

    lax.fori_loop(0, SWEEPS, sweep, 0)

    result_ref = state_ref if adjoint else field_ref

    def store(pair, carry):
        cells = join_halves([result_ref[pair, r] for r in range(ROWS)])
        for k in range(ROWS // 2):
            a, b = cells[2 * k], cells[2 * k + 1]
            out_ref[2 * pair, pl.ds(8 * k, 8), :] = jnp.where(lower, a, swap(b))
            out_ref[2 * pair + 1, pl.ds(8 * k, 8), :] = jnp.where(lower, swap(a), b)
        return carry

    lax.fori_loop(0, PAIRS, store, 0)

    if not adjoint:
        for group in range(2):
            tiles = pl.ds(8 * group, 8)
            for kind in range(2):
                start = FIELD + ROWS + kind * ROWS
                cells = split_halves([x_ref[tiles, start + c, :] for c in range(ROWS)])
                for r in range(ROWS):
                    target_ref[kind, group, r] = cells[r]
            speeds = x_ref[tiles, FIELD + 3 * ROWS, :]
            for k in range(4 * STEPS):
                speed_ref[group, k] = jnp.broadcast_to(speeds[:, k : k + 1], (8, 128))


VMEM = pl.BlockSpec(memory_space=pltpu.VMEM)
SMEM = pl.BlockSpec(memory_space=pltpu.SMEM)
BOUND = 56 * 1024 * 1024


def shape(*dims):
    return jax.ShapeDtypeStruct(dims, f32)


def smooth_forward(src, flag, received):
    return pl.pallas_call(
        functools.partial(smooth_kernel, False),
        out_shape=(
            shape(TILES, FIELD, 128),
            shape(PAIRS, ROWS, 8, 128),
            shape(2, 2, ROWS, 8, 128),
            shape(2, 4 * STEPS, 8, 128),
        ),
        in_specs=[SMEM, SMEM, VMEM],
        out_specs=(VMEM, VMEM, VMEM, VMEM),
        scratch_shapes=[
            pltpu.VMEM((PAIRS, ROWS, 8, 128), f32),
            pltpu.VMEM((2, 4 * TILES, 8, 128), f32),
        ],
        name="smooth_forward",
    )(src, flag, received)


def smooth_adjoint(src, flag, received, rate):
    return pl.pallas_call(
        functools.partial(smooth_kernel, True),
        out_shape=shape(TILES, FIELD, 128),
        in_specs=[SMEM, SMEM, VMEM, VMEM],
        out_specs=VMEM,
        scratch_shapes=[
            pltpu.VMEM((PAIRS, ROWS, 8, 128), f32),
            pltpu.VMEM((PAIRS, ROWS, 8, 128), f32),
            pltpu.VMEM((2, 4 * TILES, 8, 128), f32),
        ],
        name="smooth_adjoint",
    )(src, flag, received, rate)


def transport_kernel(
    src_ref, own_ref, flip_ref, x_ref, target_ref, speed_ref, out_ref, field_ref, strip_ref, ghost_ref, plain_ref
):
    low = iota(1) < S
    column = iota(1) % S
    mask = edge_mask()

    def save_strips(group, strips):
        for edge in range(4):
            strip_ref[pl.ds(edge * TILES + 8 * group, 8), :] = strips[edge]

    def fetch():
        for tile in range(TILES):
            for d in range(4):
                ghost_ref[pl.ds(d * TILES + tile, 1), :] = strip_ref[pl.ds(src_ref[4 * tile + d], 1), :]

    def step(section, adjoint):
        for group in range(2):
            values = [field_ref[group, r] for r in range(ROWS)]
            strips = strips_of(values[0], values[-1], column_sum(values))
            if adjoint:
                strips = [strips[d] * speed_ref[group, 4 * section + d] for d in range(4)]
            save_strips(group, strips)
        fetch()
        for group in range(2):
            c = [speed_ref[group, 4 * section + d] for d in range(4)]
            keep = 1.0 - ((c[0] + c[1]) + (c[2] + c[3]))
            tiles = [pl.ds(d * TILES + 8 * group, 8) for d in range(4)]
            ghosts = [ghost_ref[tiles[d], :] for d in range(4)]
            if not adjoint:
                ghosts = [ghosts[d] * c[d] for d in range(4)]
            else:
                c = [c[1], c[0], c[3], c[2]]
            flips = [flip_ref[tiles[d], :] for d in range(4)]
            top, bottom, sides = placed_ghosts(ghosts, flips)
            first = field_ref[group, 0]
            last = field_ref[group, ROWS - 1]
            previous = None
            here = first
            for r in range(ROWS):
                after = field_ref[group, r + 1] if r < ROWS - 1 else None
                side = turn(sides, -2 * r)
                left = jnp.where(column == 0, side, c[2] * turn(here, 1))
                right = jnp.where(column == S - 1, side, c[3] * turn(here, -1))
                if r == 0:
                    up = jnp.where(low, top, c[0] * turn(last, S))
                else:
                    up = c[0] * previous
                if r == ROWS - 1:
                    down = jnp.where(low, c[1] * turn(first, S), bottom)
                else:
                    down = c[1] * after
                new = keep * here + (up + down) + (left + right)
                if section == STEPS - 1 and not adjoint:
                    new = target_ref[0, group, r] * (new - target_ref[1, group, r])
                field_ref[group, r] = new
                previous, here = here, after

    for group in range(2):
        rows = split_halves([x_ref[pl.ds(8 * group, 8), c, :] for c in range(ROWS)])
        for r in range(ROWS):
            field_ref[group, r] = rows[r]
    for section in range(STEPS):
        step(section, False)
    for section in reversed(range(STEPS)):
        step(section, True)
    for group in range(2):
        cells = join_halves([field_ref[group, r] for r in range(ROWS)])
        for c in range(ROWS):
            plain_ref[pl.ds(8 * group, 8), c, :] = cells[c]
    mine = plain_ref[own_ref[0]]
    for other in range(out_ref.shape[0]):
        out_ref[other] = mine


def transport(src, own, flip, gathered, target, speed, copies):
    return pl.pallas_call(
        transport_kernel,
        out_shape=shape(copies, ROWS, 128),
        in_specs=[SMEM, SMEM, VMEM, VMEM, VMEM, VMEM],
        out_specs=VMEM,
        scratch_shapes=[
            pltpu.VMEM((2, ROWS, 8, 128), f32),
            pltpu.VMEM((4 * TILES, 128), f32),
            pltpu.VMEM((4 * TILES, 128), f32),
            pltpu.VMEM((TILES, ROWS, 128), f32),
        ],
        name="transport",
    )(src, own, flip, gathered, target, speed)


def exchange(values, axis):
    return lax.all_to_all(values, axis, split_axis=0, concat_axis=0, tiled=True)


def to_lines(fields):
    lead = fields.shape[:-2]
    fields = fields.reshape(*lead, L, ROWS, 128)
    return jnp.swapaxes(fields, -3, -2).reshape(*lead, FIELD, 128)


def from_lines(lines):
    lead = lines.shape[:-2]
    lines = lines.reshape(*lead, ROWS, L, 128)
    return jnp.swapaxes(lines, -3, -2).reshape(*lead, L, ROWS * 128)


def body(
    control,
    perturbations,
    diffusivity,
    flow,
    observed,
    obs_weight,
    neighbour_tile,
    neighbour_edge,
    departure,
):
    source = (neighbour_edge * TILES + neighbour_tile).reshape(-1)
    flips = (departure[:, :, 0] != 0).astype(jnp.int32) * S
    flag = flips.reshape(-1)
    flip = jnp.broadcast_to(flips.T.reshape(4 * TILES, 1), (4 * TILES, 128))
    own = lax.axis_index("tile").reshape(1)
    row = lax.axis_index("member")
    members = control.shape[0]

    control_lines = to_lines(control[:, 0])
    weight = lax.dynamic_slice_in_dim(obs_weight.reshape(V * L, ROWS * 128), row, 1, 0)
    target = lax.dynamic_slice_in_dim(observed.reshape(V * L, ROWS * 128), row, 1, 0)
    speeds = lax.dynamic_slice_in_dim(flow[:, 0], row % L, 1, 1).reshape(1, STEPS * 4)
    extra = jnp.concatenate(
        [
            diffusivity.reshape(ROWS, 128),
            weight.reshape(ROWS, 128),
            target.reshape(ROWS, 128),
            jnp.pad(speeds, ((0, 7), (0, 128 - STEPS * 4))),
        ],
        axis=0,
    )
    sent = jnp.concatenate(
        [control_lines, jnp.broadcast_to(extra[None], (members, EXTRA, 128))], axis=1
    )
    smoothed, rate, goal, speed = smooth_forward(source, flag, exchange(sent, "tile"))
    smoothed = exchange(smoothed, "tile")

    spread = to_lines(perturbations[:, 0])
    partial = jnp.sum(spread * smoothed[:, None], axis=0)
    partial = jnp.swapaxes(partial.reshape(V, ROWS, L, 128), 1, 2).reshape(V * L, ROWS, 128)
    increment = jnp.sum(exchange(partial, "member"), axis=0)
    gathered = exchange(jnp.broadcast_to(increment[None], (TILES, ROWS, 128)), "tile")
    sensitivity = exchange(transport(source, own, flip, gathered, goal, speed, V * L), "member")
    sensitivity = jnp.swapaxes(sensitivity.reshape(V, L, ROWS, 128), 1, 2).reshape(V, FIELD, 128)

    projected = jnp.sum(spread * sensitivity[None], axis=1)
    mixed = exchange(smooth_adjoint(source, flag, exchange(projected, "tile"), rate), "tile")
    return control + from_lines(mixed)[:, None]


def solution(mesh):
    in_specs = (
        P("member", "tile", None, None),
        P("member", "tile", None, None, None),
        P("tile", None),
        P(None, "tile", None, None),
        P("tile", None, None, None),
        P("tile", None, None, None),
        P(),
        P(),
        P(),
    )
    out_specs = P("member", "tile", None, None)
    return jax.shard_map(body, mesh=mesh, in_specs=in_specs, out_specs=out_specs, check_vma=False)
```

time: 552 us -> 275 us (0.50); the launches traced: 541 us -> 274 us
  local copies, waits for them, and re-layouts: 229 us -> 14.1 us
  other arithmetic: 92.6 us -> 10.7 us
  Pallas kernels: 0 us -> 60.5 us
  starting transfers between devices: 28.9 us -> 16.8 us
  waiting for transfers between devices: 88.9 us -> 80.6 us
    broadcast_in_dim x86 -> x4, local copies, waits for them, and re-layouts: 121 us -> 1.56 us  [the longest x2 0.77 us: body(): flip = jnp.broadcast_to(flips.T.reshape(4 * TILES, 1), (4 * TILES, 128))]
    slice x92 -> x0, local copies, waits for them, and re-layouts: 77.6 us -> none  [the longest x10 13.8 us: adjoint_step(): inner = inner + jnp.concatenate([parts[0][..., S:], zero_row], axis=-1)]
    pallas_call x0 -> x3, Pallas kernels: none -> 60.5 us  [the longest x1 28.4 us: smooth_forward(): pl.pallas_call(functools.partial(smooth_kernel, False), out_shape=(shape(...]
    mul x12 -> x1, other arithmetic: 41.3 us -> 0.34 us  [body(): flips = (departure[:, :, 0] != 0).astype(jnp.int32) * S]
    add x14 -> x2, other arithmetic: 35.7 us -> 1.25 us  [the longest x1 1.24 us: body(): return control + from_lines(mixed)[:, None]]
    gather x20 -> x0, local copies, waits for them, and re-layouts: 13.6 us -> none  [fetch(): jnp.take(everyone, source, axis=1).reshape(pcount, tcount, 4, qcount, S)]
    all_to_all x7 -> x3, starting transfers between devices: 28.9 us -> 16.8 us  [exchange(): return lax.all_to_all(values, axis, split_axis=0, concat_axis=0, tiled=True)]
    all_to_all x7 -> x3, waiting for transfers between devices: 88.9 us -> 80.6 us  [exchange(): return lax.all_to_all(values, axis, split_axis=0, concat_axis=0, tiled=True)]
  transfers between devices with their start and end apart: 7 -> 3, of which waited for: 7 -> 3; matrix products, arithmetic and copies ran while one was open for 1% -> 3% of each run, Pallas kernels for 0% -> 0%
where the time goes in v1:
time: 275 us; the launch traced here: 274 us
  blocking collectives  91.6 us (33%)
  waiting for transfers between devices  80.6 us (29%)
  Pallas kernels  60.5 us (22%)
  starting transfers between devices  16.8 us (6%)
  local copies, waits for them, and re-layouts  14.1 us (5%)
  other arithmetic  10.7 us (4%)
    all_to_all x4, blocking collectives, exchange(): return lax.all_to_all(values, axis, split_axis=0, concat_axis=0, tiled=True)  91.6 us
    all_to_all x3, waiting for transfers between devices, exchange(): return lax.all_to_all(values, axis, split_axis=0, concat_axis=0, tiled=True)  80.6 us
    pallas_call x1, Pallas kernels, smooth_forward(): pl.pallas_call(functools.partial(smooth_kernel, False), out_shape=(shape(...  28.4 us
    pallas_call x1, Pallas kernels, smooth_adjoint(): pl.pallas_call(functools.partial(smooth_kernel, True), out_shape=shape(TI...  28.1 us
    all_to_all x3, starting transfers between devices, exchange(): return lax.all_to_all(values, axis, split_axis=0, concat_axis=0, tiled=True)  16.8 us
    another operation x1, local copies, waits for them, and re-layouts, to_lines(): fields = fields.reshape(*lead, L, ROWS, 128)  6.06 us
  transfers between devices with their start and end apart: 3, of which 3 were waited for; matrix products, arithmetic and copies ran while one was open for 3% of the time, Pallas kernels for 0%

profile of v1, /device:TPU:2, one launch (start us, length us, event | category | flops | bytes accessed | tf_op | source)
XLA Modules:
  0.0 274.3 jit_solution(9396997269830834572)
XLA Ops:
  0.0 0.0 copy-start
  0.0 0.7 copy-done
  0.7 0.1 reshape.73
  0.8 1.0 reshape.71
  1.8 1.0 reshape.69
  2.9 0.7 select_maximum_fusion
  3.7 0.0 copy-start.5
  3.7 0.0 copy-start.6
  3.7 0.0 copy-start.4
  3.7 0.1 broadcast_in_dim.10
  3.7 2.6 pad_maximum_fusion
  6.4 9.6 %all-to-all-start = ((f32[16,232,128]{2,1,0:T(8,128)}), f32[16,232,128]{2,1,0:T(8,128)S(1)}, u32[]{:S(2)}, u32[]{:S(2)}) async-start(f32[16,232,128]{2,1,0:T(8,128)} %pad_maximum_fusion), calls=%async_computation | async-start | bytes 3801088 | tf_op jit(solution)/shard_map/all_to_all | solution.py:345
  16.0 0.0 copy-done.5
  16.0 0.0 copy-done.6
  16.0 0.1 copy.20
  16.1 0.6 reshape.65.src_ref
  16.7 0.0 copy-done.4
  16.7 0.3 fusion.2
  17.0 0.6 mul.40.flag_ref
  17.6 44.8 %all-to-all-done.x_ref = f32[16,232,128]{2,1,0:T(8,128)S(1)} async-done(((f32[16,232,128]{2,1,0:T(8,128)}), f32[16,232,128]{2,1,0:T(8,128)S(1)}, u32[]{:S(2)}, u32[]{:S(2)}) %all-to-all-start) | async-done | bytes 1900576 | tf_op jit(solution)/shard_map/all_to_all | solution.py:345
  62.4 0.0 copy-start.1
  62.4 1.3 copy-done.1
  63.7 28.4 %smooth_forward.1 = (f32[16,128,128]{2,1,0:T(8,128)}, f32[8,32,8,128]{3,2,1,0:T(8,128)}, f32[2,2,32,8,128]{4,3,2,1,0:T(8,128)}, f32[2,8,8,128]{3,2,1,0:T(8,128)}) custom-call(s32[64]{0:T(128)} %reshape.65.src_ref, s32[64]{0:T(128)} %mul.40.flag_ref, f32[16,232,128]{2,1,0:T(8,128)} %copy-done.1), custom_call_target="tpu_custom_call" | custom-call | tf_op jit(solution)/shard_map/smooth_forward/pallas_call | solution.py:220
  92.1 3.7 %all-to-all-start.1 = ((f32[16,128,128]{2,1,0:T(8,128)}), f32[16,128,128]{2,1,0:T(8,128)S(1)}, u32[]{:S(2)}, u32[]{:S(2)}) async-start(f32[16,128,128]{2,1,0:T(8,128)} %get-tuple-element.9), calls=%async_computation.1 | async-start | bytes 2097152 | tf_op jit(solution)/shard_map/all_to_all | solution.py:345
  95.7 6.1 %reshape_squeeze.6 = f32[16,4,4,32,128]{4,3,2,1,0:T(8,128)} reshape(f32[16,1,4,4,4096]{4,3,2,1,0:T(4,128)} %param.10) | data formatting | bytes 8388608 | tf_op jit(solution)/shard_map/reshape;squeeze | solution.py:350
  101.8 22.3 %all-to-all-done.1 = f32[16,128,128]{2,1,0:T(8,128)S(1)} async-done(((f32[16,128,128]{2,1,0:T(8,128)}), f32[16,128,128]{2,1,0:T(8,128)S(1)}, u32[]{:S(2)}, u32[]{:S(2)}) %all-to-all-start.1) | async-done | bytes 1048608 | tf_op jit(solution)/shard_map/all_to_all | solution.py:345
  124.1 0.1 copy.23
  124.2 2.9 %fusion = f32[4,32,4,128]{3,1,2,0:T(8,128)S(1)} fusion(f32[16,4,4,32,128]{4,3,2,1,0:T(8,128)} %reshape_squeeze.6, f32[16,32,4,128]{3,1,2,0:T(8,128)S(1)} %copy.23), kind=kLoop, calls=%fused_computation.2 | loop fusion | flops 2031616 | bytes 5505024 | tf_op jit(solution)/shard_map/reduce_sum | solution.py:399
  127.1 14.0 %all_to_all.35 = f32[16,32,128]{2,1,0:T(8,128)S(1)} all-to-all(f32[16,32,128]{2,1,0:T(8,128)S(1)} %bitcast.37), channel_id=1, replica_groups=mesh['member'=16,'tile'=16] {'member'}, dimensions={0} | all-to-all | bytes 524288 | tf_op jit(solution)/shard_map/all_to_all | solution.py:345
  141.1 0.7 broadcast_in_dim.11
  141.8 3.5 %all-to-all-start.3 = ((f32[16,32,128]{2,1,0:T(8,128)}), f32[16,32,128]{2,1,0:T(8,128)S(1)}, u32[]{:S(2)}, u32[]{:S(2)}) async-start(f32[16,32,128]{2,1,0:T(8,128)} %broadcast_in_dim.11), calls=%async_computation.3 | async-start | bytes 524288 | tf_op jit(solution)/shard_map/all_to_all | solution.py:345
  145.4 0.1 copy.21
  145.5 0.1 broadcast_in_dim.8
  145.6 13.5 %all-to-all-done.3.x_ref = f32[16,32,128]{2,1,0:T(8,128)S(1)} async-done(((f32[16,32,128]{2,1,0:T(8,128)}), f32[16,32,128]{2,1,0:T(8,128)S(1)}, u32[]{:S(2)}, u32[]{:S(2)}) %all-to-all-start.3) | async-done | bytes 262176 | tf_op jit(solution)/shard_map/all_to_all | solution.py:345
  159.0 0.0 copy-start.3
  159.0 0.7 broadcast_in_dim.9.flip_ref
  159.7 0.0 copy-done.3
  159.7 4.1 %transport.1 = f32[16,32,128]{2,1,0:T(8,128)} custom-call(s32[64]{0:T(128)} %reshape.65.src_ref, s32[1]{0:T(128)} %bitcast.1.own_ref, s32[64,128]{1,0:T(8,128)} %broadcast_in_dim.9.flip_ref, f32[16,32,128]{2,1,0:T(8,128)} %copy-done.3, f32[2,2,32,8,128]{4,3,2,1,0:T(8,128)} %get-tuple-element.10.target_ref, f32[2,8,8,128]{3,2,1,0:T(8,128)} %get-tuple-element.11.speed_ref), custom_call_target="tpu_custom_call" | custom-call | tf_op jit(solution)/shard_map/transport/pallas_call | solution.py:329
  163.8 12.0 %all_to_all.36 = f32[16,32,128]{2,1,0:T(8,128)S(1)} all-to-all(f32[16,32,128]{2,1,0:T(8,128)} %transport.1), channel_id=1, replica_groups=mesh['member'=16,'tile'=16] {'member'}, dimensions={0} | all-to-all | bytes 524288 | tf_op jit(solution)/shard_map/all_to_all | solution.py:345
  175.8 2.9 %fusion.1 = f32[16,32,4,128]{3,1,2,0:T(8,128)S(1)} fusion(f32[16,4,4,32,128]{4,3,2,1,0:T(8,128)} %reshape_squeeze.6, f32[4,32,4,128]{3,1,2,0:T(8,128)S(1)} %bitcast.36), kind=kLoop, calls=%fused_computation.3 | loop fusion | flops 1835008 | bytes 5505024 | tf_op jit(solution)/shard_map/reduce_sum | solution.py:406
  178.7 0.7 copy.24
  179.4 0.0 copy-start.2
  179.4 33.6 %all_to_all.37.x_ref = f32[16,128,128]{2,1,0:T(8,128)} all-to-all(f32[16,128,128]{2,1,0:T(8,128)S(1)} %bitcast.35), channel_id=1, replica_groups=mesh['member'=16,'tile'=16] {'tile'}, dimensions={0} | all-to-all | bytes 2097152 | tf_op jit(solution)/shard_map/all_to_all | solution.py:345
  213.0 28.1 %smooth_adjoint.1 = f32[16,128,128]{2,1,0:T(8,128)} custom-call(s32[64]{0:T(128)} %reshape.65.src_ref, s32[64]{0:T(128)} %mul.40.flag_ref, f32[16,128,128]{2,1,0:T(8,128)} %all_to_all.37.x_ref, f32[8,32,8,128]{3,2,1,0:T(8,128)} %get-tuple-element.12.refs_0_), custom_call_target="tpu_custom_call" | custom-call | tf_op jit(solution)/shard_map/smooth_adjoint/pallas_call | solution.py:239
  241.1 32.0 %all_to_all.38 = f32[16,128,128]{2,1,0:T(8,128)S(1)} all-to-all(f32[16,128,128]{2,1,0:T(8,128)} %smooth_adjoint.1), channel_id=1, replica_groups=mesh['member'=16,'tile'=16] {'tile'}, dimensions={0} | all-to-all | bytes 2097152 | tf_op jit(solution)/shard_map/all_to_all | solution.py:345
  273.1 0.0 copy-done.2
  273.1 1.2 add.23
  (4 shorter events, 0.1 us)
Async XLA Ops:
  0.0 0.7 copy-start
  3.7 12.3 %copy-start.5 = (s32[16,4]{0,1:T(4,128)S(1)}, s32[16,4]{0,1:T(4,128)}, u32[]{:S(2)}) copy-start(s32[16,4]{0,1:T(4,128)} %param.15) | copy-start | bytes 772
  3.7 12.3 %copy-start.6 = (s32[16,4]{0,1:T(4,128)S(1)}, s32[16,4]{0,1:T(4,128)}, u32[]{:S(2)}) copy-start(s32[16,4]{0,1:T(4,128)} %param.16) | copy-start | bytes 772
  3.7 13.0 %copy-start.4 = (s32[16,4,64]{2,1,0:T(4,128)S(1)}, s32[16,4,64]{2,1,0:T(4,128)}, u32[]{:S(2)}) copy-start(s32[16,4,64]{2,1,0:T(4,128)} %param.17) | copy-start | bytes 49156
  6.4 56.1 %all-to-all-start = ((f32[16,232,128]{2,1,0:T(8,128)}), f32[16,232,128]{2,1,0:T(8,128)S(1)}, u32[]{:S(2)}, u32[]{:S(2)}) async-start(f32[16,232,128]{2,1,0:T(8,128)} %pad_maximum_fusion), calls=%async_computation | async-start | bytes 3801088 | tf_op jit(solution)/shard_map/all_to_all | solution.py:345
  62.4 1.3 copy-start.1
  92.1 32.0 %all-to-all-start.1 = ((f32[16,128,128]{2,1,0:T(8,128)}), f32[16,128,128]{2,1,0:T(8,128)S(1)}, u32[]{:S(2)}, u32[]{:S(2)}) async-start(f32[16,128,128]{2,1,0:T(8,128)} %get-tuple-element.9), calls=%async_computation.1 | async-start | bytes 2097152 | tf_op jit(solution)/shard_map/all_to_all | solution.py:345
  141.8 17.2 %all-to-all-start.3 = ((f32[16,32,128]{2,1,0:T(8,128)}), f32[16,32,128]{2,1,0:T(8,128)S(1)}, u32[]{:S(2)}, u32[]{:S(2)}) async-start(f32[16,32,128]{2,1,0:T(8,128)} %broadcast_in_dim.11), calls=%async_computation.3 | async-start | bytes 524288 | tf_op jit(solution)/shard_map/all_to_all | solution.py:345
  159.0 0.7 copy-start.3
  179.4 93.7 %copy-start.2 = (f32[16,1,4,4096]{3,2,1,0:T(4,128)S(1)}, f32[16,1,4,4096]{3,2,1,0:T(4,128)}, u32[]{:S(2)}) copy-start(f32[16,1,4,4096]{3,2,1,0:T(4,128)} %param.9) | copy-start | bytes 3145732

commit v2 on v1

v2 whole, which is shorter than its diff:
```python
import functools

import jax
import jax.numpy as jnp
from jax import lax
from jax.experimental import pallas as pl
from jax.experimental.pallas import tpu as pltpu
from jax.sharding import PartitionSpec as P

S = 64
V = 4
L = 4
SWEEPS = 8
STEPS = 2
TILES = 16
PAIRS = TILES // 2
ROWS = 32
FIELD = L * ROWS
LINES = 14
FRAME = L * LINES
SERIES = 8 * SWEEPS
EXTRA = 48
f32 = jnp.float32


def iota(axis):
    return lax.broadcasted_iota(jnp.int32, (8, 128), axis)


def turn(x, shift):
    shift %= 128
    return pltpu.roll(x, shift, 1) if shift else x


def swap(x):
    return pltpu.roll(x, 4, 0)


def pick(x, index):
    return jnp.take_along_axis(x, index, axis=1, mode="promise_in_bounds")


def split_halves(cells):
    low = iota(1) < S
    out = []
    for c in range(ROWS // 2):
        first, second = cells[c], cells[c + ROWS // 2]
        out.append(jnp.where(low, first, turn(second, S)))
        out.append(jnp.where(low, turn(first, S), second))
    return out


def join_halves(rows):
    low = iota(1) < S
    out = [None] * ROWS
    for c in range(ROWS // 2):
        even, odd = rows[2 * c], rows[2 * c + 1]
        out[c] = jnp.where(low, even, turn(odd, S))
        out[c + ROWS // 2] = jnp.where(low, turn(even, S), odd)
    return out


def edge_mask():
    column = iota(1) % S
    return (column == 0) | (column == S - 1)


def column_sum(values):
    mask = edge_mask()
    parts = [turn(jnp.where(mask, values[r], 0.0), 2 * r) for r in range(ROWS)]
    while len(parts) > 1:
        parts = [a + b for a, b in zip(parts[0::2], parts[1::2])]
    return parts[0]


def strips_of(top, bottom, columns):
    lane = iota(1)
    place = jnp.where(lane < S, lane, 127 - lane)
    return (
        pick(top, place),
        pick(bottom, place + S),
        pick(columns, 2 * place),
        pick(columns, (2 * place + 63) % 128),
    )


def placed_ghosts(ghosts, flips):
    lane = iota(1)
    even = lane % 2 == 0
    along = lane % S
    top = pick(ghosts[0], along + flips[0])
    bottom = pick(ghosts[1], along + flips[1])
    left = pick(ghosts[2], lane // 2 + flips[2])
    right = pick(ghosts[3], ((lane + 65) % 128) // 2 + flips[3])
    return top, bottom, jnp.where(even, left, right)


def line_of(c):
    if c < 4:
        return c, 0
    if c >= ROWS - 4:
        return c - (ROWS - 8), 0
    block = c // 2 - 2
    return 8 + 2 * (block // 4) + c % 2, 16 * (block % 4)


def unpack(lines):
    return [turn(lines[line_of(c)[0]], -line_of(c)[1]) for c in range(ROWS)]


def gather_blocks(cells):
    lane = iota(1)
    packed = cells[0]
    for j in range(1, 4):
        packed = jnp.where((lane + 8 - 16 * j) % S < 16, turn(cells[j], 16 * j), packed)
    return packed


def pair_cells(a, b):
    lower = iota(0) < 4
    cells = []
    for x, y in zip(a, b):
        cells.append(jnp.where(lower, x, swap(y)))
        cells.append(jnp.where(lower, swap(x), y))
    return cells


def spread_row(row):
    return jnp.broadcast_to(row, (8, 128))


def pack_kernel(*refs):
    x_ref, *refs = refs
    out_ref = refs[-3] if len(refs) > 1 else refs[-1]

    def one(member, carry):
        cells = [x_ref[member, pl.ds(8 * k, 8), :] for k in range(ROWS // 2)]
        for place, k in enumerate((0, 1, 14, 15)):
            out_ref[member, pl.ds(8 * place, 8), :] = cells[k]
        for g in range(3):
            out_ref[member, pl.ds(32 + 8 * g, 8), :] = gather_blocks(cells[2 + 4 * g : 6 + 4 * g])
        return carry

    members = x_ref.shape[0]
    lax.fori_loop(0, members, one, 0, unroll=4)
    if len(refs) > 1:
        own_ref, flow_ref, rate_ref, weight_ref, target_ref, out_ref, rows_ref, pack_ref = refs
        variable, level = own_ref[0], own_ref[1]
        for c in range(ROWS):
            line = pl.ds(L * c + level, 1)
            rows_ref[0, pl.ds(c, 1), :] = rate_ref[pl.ds(c, 1), :]
            rows_ref[1, pl.ds(c, 1), :] = weight_ref[variable, line, :]
            rows_ref[2, pl.ds(c, 1), :] = target_ref[variable, line, :]
        for kind in range(3):
            base = kind * LINES
            for place, c in enumerate((0, 1, 2, 3, 28, 29, 30, 31)):
                pack_ref[pl.ds(base + place, 1), :] = rows_ref[kind, pl.ds(c, 1), :]
            for g in range(3):
                for h in range(2):
                    some = [
                        spread_row(rows_ref[kind, pl.ds(2 * (2 + 4 * g + j) + h, 1), :]) for j in range(4)
                    ]
                    pack_ref[pl.ds(base + 8 + 2 * g + h, 1), :] = gather_blocks(some)[:1]
        lane = iota(1)
        speeds = jnp.zeros((8, 128), f32)
        for k in range(4 * STEPS):
            speeds = jnp.where(lane == k, flow_ref[(k // 4 * L + level) * 4 + k % 4], speeds)
        pack_ref[pl.ds(3 * LINES, 1), :] = speeds[:1]
        pack_ref[pl.ds(3 * LINES + 1, EXTRA - 3 * LINES - 1), :] = jnp.zeros(
            (EXTRA - 3 * LINES - 1, 128), f32
        )
        for member in range(members):
            for k in range(EXTRA // 8):
                out_ref[member, pl.ds(FRAME + 8 * k, 8), :] = pack_ref[pl.ds(8 * k, 8), :]


def set_ghosts(ends, sides, first, last, seam_ref, side_ref):
    low = iota(1) < S
    for q in range(8):
        seam_ref[pl.ds(8 * q, 8), :] = jnp.where(low, ends[q], turn(last[q], S))
        seam_ref[pl.ds(S + 8 * q, 8), :] = jnp.where(low, turn(first[q], S), ends[q])
    for q in range(4):
        side_ref[pl.ds(8 * q, 8), :] = jnp.where(low, sides[q], turn(sides[q + 4], S))
        side_ref[pl.ds(ROWS + 8 * q, 8), :] = jnp.where(low, turn(sides[q], S), sides[q + 4])


def edge_rows(field_ref):
    first = [field_ref[0, pl.ds(8 * q, 8), :] for q in range(8)]
    last = [field_ref[ROWS - 1, pl.ds(8 * q, 8), :] for q in range(8)]
    return first, last


def sweep_rows(adjoint, field_ref, state_ref, rate_ref, seam_ref, side_ref):
    head, tail = iota(0) == 0, iota(0) == 7
    before = [seam_ref[pl.ds(8 * q, 8), :] for q in range(8)]
    here = [field_ref[0, pl.ds(8 * q, 8), :] for q in range(8)]
    for r in range(ROWS):
        if r < ROWS - 1:
            after = [field_ref[r + 1, pl.ds(8 * q, 8), :] for q in range(8)]
        else:
            after = [seam_ref[pl.ds(S + 8 * q, 8), :] for q in range(8)]
        outer = spread_row(side_ref[pl.ds(r, 1), :])
        down = [pltpu.roll(here[q], 1, 0) for q in range(8)]
        up = [pltpu.roll(here[q], 7, 0) for q in range(8)]
        closing = spread_row(side_ref[pl.ds(ROWS + r, 1), :])
        for q in range(8):
            cells = pl.ds(8 * q, 8)
            left = jnp.where(head, outer if q == 0 else down[q - 1], down[q])
            right = jnp.where(tail, closing if q == 7 else up[q + 1], up[q])
            change = (before[q] + after[q]) + (left + right) - 4.0 * here[q]
            if adjoint:
                state = state_ref[r, cells, :] + change
                state_ref[r, cells, :] = state
                field_ref[r, cells, :] = state * rate_ref[r, cells, :]
            else:
                field_ref[r, cells, :] = here[q] + rate_ref[r, cells, :] * change
        before, here = here, after


def scale_rows(field_ref, state_ref, rate_ref):
    def scale(r, carry):
        field_ref[r] = state_ref[r] * rate_ref[r]
        return carry

    lax.fori_loop(0, ROWS, scale, 0, unroll=4)


def pair_line(x_ref, i):
    lower = iota(0) < 4
    out = []
    for pair in range(PAIRS):
        a = x_ref[2 * pair, pl.ds(8 * (i // 2), 8), :]
        b = x_ref[2 * pair + 1, pl.ds(8 * (i // 2), 8), :]
        out.append(jnp.where(lower, a, swap(b)) if i % 2 == 0 else jnp.where(lower, swap(a), b))
    return out


def unpack_columns(line, put, get):
    low = iota(1) < S

    def turned(first, second):
        return jnp.transpose(jnp.concatenate(line(first) + line(second), axis=0))

    def part(block, start):
        start %= 128
        return block[start : start + 8]

    for c in range(4):
        block = turned(c, 4 + c)
        for parity in range(2):
            for q in range(8):
                put(2 * c + parity, q, part(block, S * parity + 8 * q))
                put(24 + 2 * c + parity, q, part(block, S * parity + 8 * q))
    starts = {(0, 0): 0, (1, 0): 64, (0, 7): 56, (1, 7): 120}
    for h in range(2):
        block = turned(8 + h, 12 + h)
        for j in range(4):
            for (parity, q), start in starts.items():
                put(8 + 4 * j + 2 * h + parity, q, part(block, start + 16 * j))
        block = turned(10 + h, 10 + h)
        for j in range(4):
            for (parity, q), start in starts.items():
                cells = part(block, start + 16 * j)
                if j < 2:
                    r = 24 + 4 * j + 2 * h + parity
                    put(r, q, jnp.where(low, cells, get(r, q)))
                else:
                    r = 4 * (j - 2) + 2 * h + parity
                    put(r, q, jnp.where(low, get(r, q), cells))


def frame_kernel(adjoint, table_ref, x_ref, *refs):
    if adjoint:
        rate_ref, out_ref, field_ref, seam_ref, side_ref, state_ref = refs
    else:
        out_ref, rate_ref, target_ref, speed_ref, field_ref, seam_ref, side_ref = refs
        state_ref = None
    lower = iota(0) < 4
    low = iota(1) < S
    zero = jnp.zeros((8, 128), f32)

    def access(ref):
        def put(r, q, value):
            ref[r, pl.ds(8 * q, 8), :] = value

        return put, lambda r, q: ref[r, pl.ds(8 * q, 8), :]

    def clear(ref):
        for r in range(8, 24):
            for q in range(1, 7):
                ref[r, pl.ds(8 * q, 8), :] = zero

    def field_line(i):
        return pair_line(x_ref, i)

    def rate_line(i):
        out = []
        for pair in range(PAIRS):
            a = x_ref[2 * pair, pl.ds(FRAME + i, 1), :]
            b = x_ref[2 * pair + 1, pl.ds(FRAME + i, 1), :]
            out.append(jnp.where(lower, spread_row(a), spread_row(b)))
        return out

    start_ref = state_ref if adjoint else field_ref
    clear(start_ref)
    unpack_columns(field_line, *access(start_ref))
    if adjoint:
        scale_rows(field_ref, state_ref, rate_ref)
    else:
        clear(rate_ref)
        unpack_columns(rate_line, *access(rate_ref))

    def place(repeat):
        first, last = edge_rows(field_ref)
        ends = [jnp.where(low, first[q], last[q]) for q in range(8)]
        left = [field_ref[pl.ds(8 * q, 8), 0, :] for q in range(4)]
        right = [field_ref[pl.ds(8 * q, 8), S - 1, :] for q in range(4)]
        sides = [jnp.where(low, left[q], turn(right[q], S)) for q in range(4)]
        sides += [jnp.where(low, turn(left[q], S), right[q]) for q in range(4)]
        mirror = 7 - iota(0)
        found = []
        for k in range(2):
            index, kind, flip = table_ref[k, 0], table_ref[k, 1], table_ref[k, 2]
            got = [jnp.where(kind != 0, pick(sides[q], index), pick(ends[q], index)) for q in range(8)]
            back = [
                jnp.take_along_axis(got[7 - q], mirror, axis=0, mode="promise_in_bounds")
                for q in range(8)
            ]
            found.append([jnp.where(flip != 0, back[q], got[q]) for q in range(8)])
        ends, sides = found
        set_ghosts(ends, sides, first, last, seam_ref, side_ref)
        block = jnp.transpose(jnp.concatenate(ends + sides, axis=0))
        line = pl.ds(pl.multiple_of(8 * repeat, 8), 8)
        for pair in range(PAIRS):
            a = block[8 * pair : 8 * pair + 8]
            b = block[S + 8 * pair : S + 8 * pair + 8]
            out_ref[2 * pair, line, :] = jnp.where(lower, a, swap(b))
            out_ref[2 * pair + 1, line, :] = jnp.where(lower, swap(a), b)

    def sweep(repeat, carry):
        place(repeat)
        sweep_rows(adjoint, field_ref, state_ref, rate_ref, seam_ref, side_ref)
        return carry

    lax.fori_loop(0, SWEEPS - 1, sweep, 0)
    place(SWEEPS - 1)

    if not adjoint:
        for group in range(2):
            tiles = pl.ds(8 * group, 8)
            for kind in range(2):
                start = FRAME + LINES + kind * LINES
                cells = split_halves(unpack([x_ref[tiles, start + i, :] for i in range(LINES)]))
                for r in range(ROWS):
                    target_ref[kind, group, r] = cells[r]
            speeds = x_ref[tiles, FRAME + 3 * LINES, :]
            for k in range(4 * STEPS):
                speed_ref[group, k] = jnp.broadcast_to(speeds[:, k : k + 1], (8, 128))


def load_columns(line, ref):
    for c in range(ROWS // 2):
        block = jnp.transpose(jnp.concatenate(line(c) + line(c + ROWS // 2), axis=0))
        for parity in range(2):
            ref[2 * c + parity] = block[S * parity : S * parity + S]


def rate_kernel(rows_ref, out_ref):
    load_columns(lambda c: [spread_row(rows_ref[0, pl.ds(c, 1), :])] * PAIRS, out_ref)


def tile_kernel(adjoint, x_ref, series_ref, rate_ref, *refs):
    if adjoint:
        added_ref, out_ref, field_ref, seam_ref, side_ref, state_ref = refs
    else:
        out_ref, field_ref, seam_ref, side_ref = refs
        state_ref = None
    lower = iota(0) < 4
    result_ref = state_ref if adjoint else field_ref
    load_columns(lambda c: pair_line(x_ref, c), result_ref)
    if adjoint:
        scale_rows(field_ref, state_ref, rate_ref)

    def sweep(repeat, carry):
        line = pl.ds(pl.multiple_of(8 * repeat, 8), 8)
        near, far = [], []
        for pair in range(PAIRS):
            one, other = pair_cells([series_ref[2 * pair, line, :]], [series_ref[2 * pair + 1, line, :]])
            near.append(one)
            far.append(other)
        block = jnp.transpose(jnp.concatenate(near + far, axis=0))
        ends = [block[8 * q : 8 * q + 8] for q in range(8)]
        sides = [block[S + 8 * q : S + 8 * q + 8] for q in range(8)]
        set_ghosts(ends, sides, *edge_rows(field_ref), seam_ref, side_ref)
        sweep_rows(adjoint, field_ref, state_ref, rate_ref, seam_ref, side_ref)
        return carry

    lax.fori_loop(0, SWEEPS, sweep, 0)

    for k in range(ROWS // 4):
        even, odd = [
            jnp.transpose(jnp.concatenate([result_ref[2 * c], result_ref[2 * c + 1]], axis=0))
            for c in (2 * k, 2 * k + 1)
        ]
        for half in range(2):
            line = pl.ds(8 * k + FIELD // 2 * half, 8)
            for pair in range(PAIRS):
                start = S * half + 8 * pair
                a, b = even[start : start + 8], odd[start : start + 8]
                a, b = jnp.where(lower, a, swap(b)), jnp.where(lower, swap(a), b)
                if adjoint:
                    a = a + added_ref[2 * pair, line, :]
                    b = b + added_ref[2 * pair + 1, line, :]
                out_ref[2 * pair, line, :] = a
                out_ref[2 * pair + 1, line, :] = b


VMEM = pl.BlockSpec(memory_space=pltpu.VMEM)
SMEM = pl.BlockSpec(memory_space=pltpu.SMEM)


def shape(*dims):
    return jax.ShapeDtypeStruct(dims, f32)


def pack_first(lines, own, flow, rate, weight, target):
    return pl.pallas_call(
        pack_kernel,
        out_shape=(shape(lines.shape[0], FRAME + EXTRA, 128), shape(3, ROWS, 128)),
        in_specs=[VMEM, SMEM, SMEM, VMEM, VMEM, VMEM],
        out_specs=(VMEM, VMEM),
        scratch_shapes=[pltpu.VMEM((EXTRA, 128), f32)],
        name="pack_first",
    )(lines, own, flow, rate, weight, target)


def pack(lines):
    return pl.pallas_call(
        pack_kernel,
        out_shape=shape(lines.shape[0], FRAME, 128),
        in_specs=[VMEM],
        out_specs=VMEM,
        name="pack",
    )(lines)


FIELDS = pltpu.VMEM((ROWS, S, 128), f32)
FRAME_SCRATCH = [FIELDS, pltpu.VMEM((2 * S, 128), f32), pltpu.VMEM((2 * ROWS, 128), f32)]


def frame_forward(table, received):
    return pl.pallas_call(
        functools.partial(frame_kernel, False),
        out_shape=(
            shape(TILES, SERIES, 128),
            shape(ROWS, S, 128),
            shape(2, 2, ROWS, 8, 128),
            shape(2, 4 * STEPS, 8, 128),
        ),
        in_specs=[VMEM, VMEM],
        out_specs=(VMEM, VMEM, VMEM, VMEM),
        scratch_shapes=FRAME_SCRATCH,
        name="frame_forward",
    )(table, received)


def frame_adjoint(table, received, rate):
    return pl.pallas_call(
        functools.partial(frame_kernel, True),
        out_shape=shape(TILES, SERIES, 128),
        in_specs=[VMEM, VMEM, VMEM],
        out_specs=VMEM,
        scratch_shapes=FRAME_SCRATCH + [FIELDS],
        name="frame_adjoint",
    )(table, received, rate)


def spread_rate(rows):
    return pl.pallas_call(
        rate_kernel,
        out_shape=shape(ROWS, S, 128),
        in_specs=[VMEM],
        out_specs=VMEM,
        cost_estimate=pl.CostEstimate(flops=2_000_000, bytes_accessed=1_100_000, transcendentals=0),
        name="spread_rate",
    )(rows)


def tile_smooth(adjoint, lines, series, rate, *added):
    return pl.pallas_call(
        functools.partial(tile_kernel, adjoint),
        out_shape=shape(lines.shape[0], FIELD, 128),
        in_specs=[VMEM] * (3 + len(added)),
        out_specs=VMEM,
        scratch_shapes=FRAME_SCRATCH + [FIELDS] * adjoint,
        name="tile_adjoint" if adjoint else "tile_forward",
    )(lines, series, rate, *added)


def transport_kernel(
    src_ref,
    own_ref,
    flip_ref,
    x_ref,
    target_ref,
    speed_ref,
    rows_ref,
    out_ref,
    field_ref,
    strip_ref,
    ghost_ref,
    plain_ref,
    mine_ref,
):
    low = iota(1) < S
    column = iota(1) % S
    mask = edge_mask()

    def save_strips(group, strips):
        for edge in range(4):
            strip_ref[pl.ds(edge * TILES + 8 * group, 8), :] = strips[edge]

    def fetch():
        for tile in range(TILES):
            for d in range(4):
                ghost_ref[pl.ds(d * TILES + tile, 1), :] = strip_ref[pl.ds(src_ref[4 * tile + d], 1), :]

    def step(section, adjoint):
        for group in range(2):
            values = [field_ref[group, r] for r in range(ROWS)]
            strips = strips_of(values[0], values[-1], column_sum(values))
            if adjoint:
                strips = [strips[d] * speed_ref[group, 4 * section + d] for d in range(4)]
            save_strips(group, strips)
        fetch()
        for group in range(2):
            c = [speed_ref[group, 4 * section + d] for d in range(4)]
            keep = 1.0 - ((c[0] + c[1]) + (c[2] + c[3]))
            tiles = [pl.ds(d * TILES + 8 * group, 8) for d in range(4)]
            ghosts = [ghost_ref[tiles[d], :] for d in range(4)]
            if not adjoint:
                ghosts = [ghosts[d] * c[d] for d in range(4)]
            else:
                c = [c[1], c[0], c[3], c[2]]
            flips = [flip_ref[tiles[d], :] for d in range(4)]
            top, bottom, sides = placed_ghosts(ghosts, flips)
            first = field_ref[group, 0]
            last = field_ref[group, ROWS - 1]
            owned = iota(0) + 8 * group == own_ref[0]
            previous = None
            here = first
            for r in range(ROWS):
                after = field_ref[group, r + 1] if r < ROWS - 1 else None
                side = turn(sides, -2 * r)
                left = jnp.where(column == 0, side, c[2] * turn(here, 1))
                right = jnp.where(column == S - 1, side, c[3] * turn(here, -1))
                if r == 0:
                    up = jnp.where(low, top, c[0] * turn(last, S))
                else:
                    up = c[0] * previous
                if r == ROWS - 1:
                    down = jnp.where(low, c[1] * turn(first, S), bottom)
                else:
                    down = c[1] * after
                new = keep * here + (up + down) + (left + right)
                if section == STEPS - 1 and not adjoint:
                    weight = jnp.where(owned, mine_ref[0, r], target_ref[0, group, r])
                    goal = jnp.where(owned, mine_ref[1, r], target_ref[1, group, r])
                    new = weight * (new - goal)
                field_ref[group, r] = new
                previous, here = here, after

    for kind in range(2):
        rows = split_halves([spread_row(rows_ref[kind + 1, pl.ds(c, 1), :]) for c in range(ROWS)])
        for r in range(ROWS):
            mine_ref[kind, r] = rows[r]
    for group in range(2):
        rows = split_halves([x_ref[pl.ds(8 * group, 8), c, :] for c in range(ROWS)])
        for r in range(ROWS):
            field_ref[group, r] = rows[r]
    for section in range(STEPS):
        step(section, False)
    for section in reversed(range(STEPS)):
        step(section, True)
    for group in range(2):
        cells = join_halves([field_ref[group, r] for r in range(ROWS)])
        for c in range(ROWS):
            plain_ref[pl.ds(8 * group, 8), c, :] = cells[c]
    mine = plain_ref[own_ref[0]]
    for other in range(out_ref.shape[0]):
        out_ref[other] = mine


def transport(src, own, flip, gathered, target, speed, rows, copies):
    return pl.pallas_call(
        transport_kernel,
        out_shape=shape(copies, ROWS, 128),
        in_specs=[SMEM, SMEM] + [VMEM] * 5,
        out_specs=VMEM,
        scratch_shapes=[
            pltpu.VMEM((2, ROWS, 8, 128), f32),
            pltpu.VMEM((4 * TILES, 128), f32),
            pltpu.VMEM((4 * TILES, 128), f32),
            pltpu.VMEM((TILES, ROWS, 128), f32),
            pltpu.VMEM((2, ROWS, 8, 128), f32),
        ],
        name="transport",
    )(src, own, flip, gathered, target, speed, rows)


def exchange(values, axis):
    return lax.all_to_all(values, axis, split_axis=0, concat_axis=0, tiled=True)


def to_lines(fields):
    lead = fields.shape[:-2]
    fields = fields.reshape(*lead, L, ROWS, 128)
    return jnp.swapaxes(fields, -3, -2).reshape(*lead, FIELD, 128)


def from_lines(lines):
    lead = lines.shape[:-2]
    lines = lines.reshape(*lead, ROWS, L, 128)
    return jnp.swapaxes(lines, -3, -2).reshape(*lead, L, ROWS * 128)


def body(
    control,
    perturbations,
    diffusivity,
    flow,
    observed,
    obs_weight,
    neighbour_tile,
    neighbour_edge,
    departure,
):
    source = (neighbour_edge * TILES + neighbour_tile).reshape(-1)
    flips = (departure[:, :, 0] != 0).astype(jnp.int32) * S

    def by_lane(values):
        return jnp.repeat(values.T.reshape(2, 2 * TILES), L, axis=1)

    place = (neighbour_edge % 2) * S + neighbour_tile * L
    index = by_lane(place) + jnp.arange(128, dtype=jnp.int32) % L
    table = jnp.stack([index, by_lane(neighbour_edge // 2), by_lane(flips)], axis=1)
    table = jnp.broadcast_to(table[:, :, None], (2, 3, 8, 128))
    flip = jnp.broadcast_to(flips.T.reshape(4 * TILES, 1), (4 * TILES, 128))
    own = lax.axis_index("tile").reshape(1)
    row = lax.axis_index("member")
    control_lines = to_lines(control[:, 0])

    packed, rows = pack_first(
        control_lines,
        jnp.stack([row // L, row % L]),
        flow.reshape(-1),
        diffusivity.reshape(ROWS, 128),
        to_lines(obs_weight[0]),
        to_lines(observed[0]),
    )
    own_rate = spread_rate(rows)
    received = exchange(packed, "tile")
    series, rate, goal, speed = frame_forward(table, received)
    smoothed = tile_smooth(False, control_lines, exchange(series, "tile"), own_rate)

    spread = to_lines(perturbations[:, 0])
    partial = jnp.sum(spread * smoothed[:, None], axis=0)
    partial = jnp.swapaxes(partial.reshape(V, ROWS, L, 128), 1, 2).reshape(V * L, ROWS, 128)
    increment = jnp.sum(exchange(partial, "member"), axis=0)
    gathered = exchange(jnp.broadcast_to(increment[None], (TILES, ROWS, 128)), "tile")
    sensitivity = transport(source, own, flip, gathered, goal, speed, rows, V * L)
    sensitivity = exchange(sensitivity, "member")
    sensitivity = jnp.swapaxes(sensitivity.reshape(V, L, ROWS, 128), 1, 2).reshape(V, FIELD, 128)

    projected = jnp.sum(spread * sensitivity[None], axis=1)
    series = frame_adjoint(table, exchange(pack(projected), "tile"), rate)
    mixed = tile_smooth(True, projected, exchange(series, "tile"), own_rate, control_lines)
    return from_lines(mixed)[:, None]


def solution(mesh):
    in_specs = (
        P("member", "tile", None, None),
        P("member", "tile", None, None, None),
        P("tile", None),
        P(None, "tile", None, None),
        P("tile", None, None, None),
        P("tile", None, None, None),
        P(),
        P(),
        P(),
    )
    out_specs = P("member", "tile", None, None)
    return jax.shard_map(body, mesh=mesh, in_specs=in_specs, out_specs=out_specs, check_vma=False)
```

time: 275 us -> 194 us (0.71)
  waiting for transfers between devices: 80.6 us -> 43.3 us
  blocking collectives: 91.6 us -> 69.3 us
  Pallas kernels: 60.5 us -> 40.3 us
  other arithmetic: 10.7 us -> 7.88 us
    all_to_all x3, waiting for transfers between devices: 80.6 us -> 43.3 us  [exchange(): return lax.all_to_all(values, axis, split_axis=0, concat_axis=0, tiled=True)]
    all_to_all x4, blocking collectives: 91.6 us -> 69.3 us  [exchange(): return lax.all_to_all(values, axis, split_axis=0, concat_axis=0, tiled=True)]
    pallas_call x2 -> x7, Pallas kernels: 56.4 us -> 35.5 us  [the longest x2 14.2 us: tile_smooth(): pl.pallas_call(functools.partial(tile_kernel, adjoint), out_shape=shape(l...]
    concatenate x2 -> x0, other arithmetic: 3.35 us -> none  [the longest x1 2.62 us: body(): jnp.concatenate([control_lines, jnp.broadcast_to(extra[None], (members, E...]
  transfers between devices with their start and end apart: 3 -> 3, of which waited for: 3 -> 3; matrix products, arithmetic and copies ran while one was open for 3% -> 5% of each run, Pallas kernels for 0% -> 1%
where the time goes in v2:
time: 194 us; the launch traced here: 193 us
  blocking collectives  69.3 us (36%)
  waiting for transfers between devices  43.3 us (22%)
  Pallas kernels  40.3 us (21%)
  starting transfers between devices  16.7 us (9%)
  local copies, waits for them, and re-layouts  15.3 us (8%)
  other arithmetic  7.88 us (4%)
    all_to_all x4, blocking collectives, exchange(): return lax.all_to_all(values, axis, split_axis=0, concat_axis=0, tiled=True)  69.3 us
    all_to_all x3, waiting for transfers between devices, exchange(): return lax.all_to_all(values, axis, split_axis=0, concat_axis=0, tiled=True)  43.3 us
    all_to_all x3, starting transfers between devices, exchange(): return lax.all_to_all(values, axis, split_axis=0, concat_axis=0, tiled=True)  16.7 us
    pallas_call x2, Pallas kernels, tile_smooth(): pl.pallas_call(functools.partial(tile_kernel, adjoint), out_shape=shape(l...  14.2 us
    pallas_call x1, Pallas kernels, frame_forward(): pl.pallas_call(functools.partial(frame_kernel, False), out_shape=(shape(T...  6.97 us
    pallas_call x1, Pallas kernels, frame_adjoint(): pl.pallas_call(functools.partial(frame_kernel, True), out_shape=shape(TIL...  6.85 us
    another operation x1, local copies, waits for them, and re-layouts, to_lines(): fields = fields.reshape(*lead, L, ROWS, 128)  6.07 us
    pallas_call x1, Pallas kernels, transport(): pl.pallas_call(transport_kernel, out_shape=shape(copies, ROWS, 128), in_s...  4.85 us
  transfers between devices with their start and end apart: 3, of which 3 were waited for; matrix products, arithmetic and copies ran while one was open for 5% of the time, Pallas kernels for 1%

profile of v2, /device:TPU:2, one launch (start us, length us, event | category | flops | bytes accessed | tf_op | source)
XLA Modules:
  0.0 192.9 jit_solution(3740356235551846106)
XLA Ops:
  0.0 1.3 reshape.106.refs_2_
  1.3 0.6 pad_add_fusion.1.refs_1_
  1.9 2.8 %pack_first.1 = (f32[16,104,128]{2,1,0:T(8,128)}, f32[3,32,128]{2,1,0:T(8,128)}) custom-call(f32[16,128,128]{2,1,0:T(8,128)} %bitcast.46, s32[2]{0:T(128)} %pad_add_fusion.1.refs_1_, f32[32]{0:T(128)} %reshape.106.refs_2_, f32[32,128]{1,0:T(8,128)} %bitcast.58, f32[4,128,128]{2,1,0:T(8,128)} %bitcast.54, f32[4,128,128]{2,1,0:T(8,128)} %bitcast.55), custom_call_target="tpu_custom_call" | custom-call | tf_op jit(solution)/shard_map/pack_first/pallas_call | solution.py:427
  4.8 9.6 %all-to-all-start = ((f32[16,104,128]{2,1,0:T(8,128)}), f32[16,104,128]{2,1,0:T(8,128)S(1)}, u32[]{:S(2)}, u32[]{:S(2)}) async-start(f32[16,104,128]{2,1,0:T(8,128)} %get-tuple-element.11), calls=%async_computation | async-start | bytes 1703936 | tf_op jit(solution)/shard_map/all_to_all | solution.py:612
  14.3 0.7 fusion.5
  15.1 0.1 reshape.102
  15.1 0.1 broadcast_in_dim.32
  15.2 0.1 reshape.103
  15.3 0.1 reshape.104
  15.4 0.1 broadcast_in_dim.33
  15.5 0.1 stack_reshape.6
  15.6 0.8 fusion.2
  16.4 0.1 copy.26
  16.5 0.1 reshape.105
  16.6 0.1 broadcast_in_dim.34
  16.6 0.1 stack_reshape.7
  16.8 22.0 %all-to-all-done.x_ref = f32[16,104,128]{2,1,0:T(8,128)S(1)} async-done(((f32[16,104,128]{2,1,0:T(8,128)}), f32[16,104,128]{2,1,0:T(8,128)S(1)}, u32[]{:S(2)}, u32[]{:S(2)}) %all-to-all-start) | async-done | bytes 852000 | tf_op jit(solution)/shard_map/all_to_all | solution.py:612
  38.8 0.0 copy-start
  38.8 0.6 broadcast_in_dim.35.table_ref
  39.4 0.3 copy-done
  39.7 7.0 %frame_forward.1 = (f32[16,64,128]{2,1,0:T(8,128)}, f32[32,64,128]{2,1,0:T(8,128)}, f32[2,2,32,8,128]{4,3,2,1,0:T(8,128)}, f32[2,8,8,128]{3,2,1,0:T(8,128)}) custom-call(s32[2,3,8,128]{3,2,1,0:T(8,128)} %broadcast_in_dim.35.table_ref, f32[16,104,128]{2,1,0:T(8,128)} %copy-done), custom_call_target="tpu_custom_call" | custom-call | tf_op jit(solution)/shard_map/frame_forward/pallas_call | solution.py:452
  46.7 3.6 %all-to-all-start.1 = ((f32[16,64,128]{2,1,0:T(8,128)}), f32[16,64,128]{2,1,0:T(8,128)S(1)}, u32[]{:S(2)}, u32[]{:S(2)}) async-start(f32[16,64,128]{2,1,0:T(8,128)} %get-tuple-element.12), calls=%async_computation.1 | async-start | bytes 1048576 | tf_op jit(solution)/shard_map/all_to_all | solution.py:612
  50.3 6.1 %reshape_squeeze.12 = f32[16,4,4,32,128]{4,3,2,1,0:T(8,128)} reshape(f32[16,1,4,4,4096]{4,3,2,1,0:T(4,128)} %param.10) | data formatting | bytes 8388608 | tf_op jit(solution)/shard_map/reshape;squeeze | solution.py:617
  56.3 2.1 %spread_rate.1.rate_ref = f32[32,64,128]{2,1,0:T(8,128)} custom-call(f32[3,32,128]{2,1,0:T(8,128)} %get-tuple-element.13.rows_ref), custom_call_target="tpu_custom_call" | custom-call | flops 2000000 | bytes 1100000 | tf_op jit(solution)/shard_map/spread_rate/pallas_call | solution.py:479
  58.4 8.5 %all-to-all-done.1.series_ref = f32[16,64,128]{2,1,0:T(8,128)S(1)} async-done(((f32[16,64,128]{2,1,0:T(8,128)}), f32[16,64,128]{2,1,0:T(8,128)S(1)}, u32[]{:S(2)}, u32[]{:S(2)}) %all-to-all-start.1) | async-done | bytes 524320 | tf_op jit(solution)/shard_map/all_to_all | solution.py:612
  66.9 0.0 copy-start.1
  66.9 0.8 copy-done.1
  67.7 6.8 %tile_forward.1 = f32[16,128,128]{2,1,0:T(8,128)} custom-call(f32[16,128,128]{2,1,0:T(8,128)} %bitcast.47, f32[16,64,128]{2,1,0:T(8,128)} %copy-done.1, f32[32,64,128]{2,1,0:T(8,128)} %spread_rate.1.rate_ref), custom_call_target="tpu_custom_call" | custom-call | tf_op jit(solution)/shard_map/tile_forward/pallas_call | solution.py:490
  74.5 1.3 copy.31
  75.9 2.9 %fusion = f32[4,32,4,128]{3,1,2,0:T(8,128)S(1)} fusion(f32[16,4,4,32,128]{4,3,2,1,0:T(8,128)} %reshape_squeeze.12, f32[16,32,4,128]{3,1,2,0:T(8,128)S(1)} %copy.31), kind=kLoop, calls=%fused_computation.2 | loop fusion | flops 2031616 | bytes 5505024 | tf_op jit(solution)/shard_map/reduce_sum | solution.py:667
  78.7 14.0 %all_to_all.35 = f32[16,32,128]{2,1,0:T(8,128)S(1)} all-to-all(f32[16,32,128]{2,1,0:T(8,128)S(1)} %bitcast.53), channel_id=1, replica_groups=mesh['member'=16,'tile'=16] {'member'}, dimensions={0} | all-to-all | bytes 524288 | tf_op jit(solution)/shard_map/all_to_all | solution.py:612
  92.7 0.7 broadcast_in_dim.36
  93.4 3.5 %all-to-all-start.3 = ((f32[16,32,128]{2,1,0:T(8,128)}), f32[16,32,128]{2,1,0:T(8,128)S(1)}, u32[]{:S(2)}, u32[]{:S(2)}) async-start(f32[16,32,128]{2,1,0:T(8,128)} %broadcast_in_dim.36), calls=%async_computation.3 | async-start | bytes 524288 | tf_op jit(solution)/shard_map/all_to_all | solution.py:612
  97.0 0.1 broadcast_in_dim.14
  97.1 0.1 copy.25
  97.1 0.7 reshape.99.src_ref
  97.8 12.8 %all-to-all-done.3.x_ref = f32[16,32,128]{2,1,0:T(8,128)S(1)} async-done(((f32[16,32,128]{2,1,0:T(8,128)}), f32[16,32,128]{2,1,0:T(8,128)S(1)}, u32[]{:S(2)}, u32[]{:S(2)}) %all-to-all-start.3) | async-done | bytes 262176 | tf_op jit(solution)/shard_map/all_to_all | solution.py:612
  110.6 0.7 broadcast_in_dim.15.flip_ref
  111.3 0.0 copy-done.2
  111.3 4.9 %transport.1 = f32[16,32,128]{2,1,0:T(8,128)} custom-call(s32[64]{0:T(128)} %reshape.99.src_ref, s32[1]{0:T(128)} %bitcast.1.own_ref, s32[64,128]{1,0:T(8,128)} %broadcast_in_dim.15.flip_ref, f32[16,32,128]{2,1,0:T(8,128)} %copy-done.2, f32[2,2,32,8,128]{4,3,2,1,0:T(8,128)} %get-tuple-element.14.target_ref, f32[2,8,8,128]{3,2,1,0:T(8,128)} %get-tuple-element.15.speed_ref, ...), custom_call_target="tpu_custom_call" | custom-call | tf_op jit(solution)/shard_map/transport/pallas_call | solution.py:595
  116.2 12.0 %all_to_all.36 = f32[16,32,128]{2,1,0:T(8,128)S(1)} all-to-all(f32[16,32,128]{2,1,0:T(8,128)} %transport.1), channel_id=1, replica_groups=mesh['member'=16,'tile'=16] {'member'}, dimensions={0} | all-to-all | bytes 524288 | tf_op jit(solution)/shard_map/all_to_all | solution.py:612
  128.2 2.9 %fusion.1 = f32[16,32,4,128]{3,1,2,0:T(8,128)S(1)} fusion(f32[16,4,4,32,128]{4,3,2,1,0:T(8,128)} %reshape_squeeze.12, f32[4,32,4,128]{3,1,2,0:T(8,128)S(1)} %bitcast.52), kind=kLoop, calls=%fused_computation.3 | loop fusion | flops 1835008 | bytes 5505024 | tf_op jit(solution)/shard_map/reduce_sum | solution.py:675
  131.1 1.7 copy.32
  132.7 2.4 %pack.1 = f32[16,56,128]{2,1,0:T(8,128)} custom-call(f32[16,128,128]{2,1,0:T(8,128)} %bitcast.49), custom_call_target="tpu_custom_call" | custom-call | tf_op jit(solution)/shard_map/pack/pallas_call | solution.py:438
  135.2 21.9 %all_to_all.37.x_ref = f32[16,56,128]{2,1,0:T(8,128)} all-to-all(f32[16,56,128]{2,1,0:T(8,128)} %pack.1), channel_id=1, replica_groups=mesh['member'=16,'tile'=16] {'tile'}, dimensions={0} | all-to-all | bytes 917504 | tf_op jit(solution)/shard_map/all_to_all | solution.py:612
  157.0 6.9 %frame_adjoint.1 = f32[16,64,128]{2,1,0:T(8,128)} custom-call(s32[2,3,8,128]{3,2,1,0:T(8,128)} %broadcast_in_dim.35.table_ref, f32[16,56,128]{2,1,0:T(8,128)} %all_to_all.37.x_ref, f32[32,64,128]{2,1,0:T(8,128)} %get-tuple-element.16.refs_0_), custom_call_target="tpu_custom_call" | custom-call | tf_op jit(solution)/shard_map/frame_adjoint/pallas_call | solution.py:468
  163.9 21.5 %all_to_all.38.series_ref = f32[16,64,128]{2,1,0:T(8,128)} all-to-all(f32[16,64,128]{2,1,0:T(8,128)} %frame_adjoint.1), channel_id=1, replica_groups=mesh['member'=16,'tile'=16] {'tile'}, dimensions={0} | all-to-all | bytes 1048576 | tf_op jit(solution)/shard_map/all_to_all | solution.py:612
  185.4 7.4 %tile_adjoint.1 = f32[16,128,128]{2,1,0:T(8,128)} custom-call(f32[16,128,128]{2,1,0:T(8,128)} %bitcast.50, f32[16,64,128]{2,1,0:T(8,128)} %all_to_all.38.series_ref, f32[32,64,128]{2,1,0:T(8,128)} %spread_rate.1.rate_ref, f32[16,128,128]{2,1,0:T(8,128)} %bitcast.48), custom_call_target="tpu_custom_call" | custom-call | tf_op jit(solution)/shard_map/tile_adjoint/pallas_call | solution.py:490
  (6 shorter events, 0.0 us)
Async XLA Ops:
  4.8 34.0 %all-to-all-start = ((f32[16,104,128]{2,1,0:T(8,128)}), f32[16,104,128]{2,1,0:T(8,128)S(1)}, u32[]{:S(2)}, u32[]{:S(2)}) async-start(f32[16,104,128]{2,1,0:T(8,128)} %get-tuple-element.11), calls=%async_computation | async-start | bytes 1703936 | tf_op jit(solution)/shard_map/all_to_all | solution.py:612
  38.8 0.9 copy-start
  46.7 20.2 %all-to-all-start.1 = ((f32[16,64,128]{2,1,0:T(8,128)}), f32[16,64,128]{2,1,0:T(8,128)S(1)}, u32[]{:S(2)}, u32[]{:S(2)}) async-start(f32[16,64,128]{2,1,0:T(8,128)} %get-tuple-element.12), calls=%async_computation.1 | async-start | bytes 1048576 | tf_op jit(solution)/shard_map/all_to_all | solution.py:612
  66.9 0.8 copy-start.1
  93.4 17.2 %all-to-all-start.3 = ((f32[16,32,128]{2,1,0:T(8,128)}), f32[16,32,128]{2,1,0:T(8,128)S(1)}, u32[]{:S(2)}, u32[]{:S(2)}) async-start(f32[16,32,128]{2,1,0:T(8,128)} %broadcast_in_dim.36), calls=%async_computation.3 | async-start | bytes 524288 | tf_op jit(solution)/shard_map/all_to_all | solution.py:612
  110.6 0.7 copy-start.2

commit v3 on v2

--- a/solution.py
+++ b/solution.py
@@ -15,11 +15,13 @@
 TILES = 16
 PAIRS = TILES // 2
 ROWS = 32
+GROUP = 4
 FIELD = L * ROWS
 LINES = 14
 FRAME = L * LINES
 SERIES = 8 * SWEEPS
-EXTRA = 48
+SHALLOW = 4
+EXTRA = 24
 f32 = jnp.float32
 
 
@@ -95,25 +97,26 @@
     return top, bottom, jnp.where(even, left, right)
 
 
-def line_of(c):
-    if c < 4:
-        return c, 0
-    if c >= ROWS - 4:
-        return c - (ROWS - 8), 0
-    block = c // 2 - 2
-    return 8 + 2 * (block // 4) + c % 2, 16 * (block % 4)
-
-
-def unpack(lines):
-    return [turn(lines[line_of(c)[0]], -line_of(c)[1]) for c in range(ROWS)]
-
-
 def gather_blocks(cells):
     lane = iota(1)
     packed = cells[0]
     for j in range(1, 4):
         packed = jnp.where((lane + 8 - 16 * j) % S < 16, turn(cells[j], 16 * j), packed)
     return packed
+
+
+def gather_corners(cells):
+    lane = iota(1)
+    packed = cells[0]
+    for j in range(1, 16):
+        packed = jnp.where((lane + 2 - 4 * j) % S < 4, turn(cells[j], 4 * j), packed)
+    return packed
+
+
+def unpack_shallow(lines):
+    out = [turn(lines[2 + c // 16], -4 * (c % 16)) for c in range(ROWS)]
+    out[0], out[-1] = lines[0], lines[1]
+    return out
 
 
 def pair_cells(a, b):
@@ -129,49 +132,97 @@
     return jnp.broadcast_to(row, (8, 128))
 
 
-def pack_kernel(*refs):
-    x_ref, *refs = refs
-    out_ref = refs[-3] if len(refs) > 1 else refs[-1]
+def pack_frame(cells, out_ref, member):
+    for place, k in enumerate((0, 1, 14, 15)):
+        out_ref[member, pl.ds(8 * place, 8), :] = cells[k]
+    for g in range(3):
+        out_ref[member, pl.ds(32 + 8 * g, 8), :] = gather_blocks(cells[2 + 4 * g : 6 + 4 * g])
+
+
+def pack_kernel(x_ref, flow_ref, rate_ref, weight_ref, target_ref, out_ref, rows_ref, pack_ref):
+    members = x_ref.shape[0]
 
     def one(member, carry):
         cells = [x_ref[member, pl.ds(8 * k, 8), :] for k in range(ROWS // 2)]
-        for place, k in enumerate((0, 1, 14, 15)):
-            out_ref[member, pl.ds(8 * place, 8), :] = cells[k]
-        for g in range(3):
-            out_ref[member, pl.ds(32 + 8 * g, 8), :] = gather_blocks(cells[2 + 4 * g : 6 + 4 * g])
+        pack_frame(cells, out_ref, member)
         return carry
 
-    members = x_ref.shape[0]
-    lax.fori_loop(0, members, one, 0, unroll=4)
-    if len(refs) > 1:
-        own_ref, flow_ref, rate_ref, weight_ref, target_ref, out_ref, rows_ref, pack_ref = refs
-        variable, level = own_ref[0], own_ref[1]
-        for c in range(ROWS):
-            line = pl.ds(L * c + level, 1)
-            rows_ref[0, pl.ds(c, 1), :] = rate_ref[pl.ds(c, 1), :]
-            rows_ref[1, pl.ds(c, 1), :] = weight_ref[variable, line, :]
-            rows_ref[2, pl.ds(c, 1), :] = target_ref[variable, line, :]
-        for kind in range(3):
-            base = kind * LINES
-            for place, c in enumerate((0, 1, 2, 3, 28, 29, 30, 31)):
-                pack_ref[pl.ds(base + place, 1), :] = rows_ref[kind, pl.ds(c, 1), :]
-            for g in range(3):
-                for h in range(2):
-                    some = [
-                        spread_row(rows_ref[kind, pl.ds(2 * (2 + 4 * g + j) + h, 1), :]) for j in range(4)
-                    ]
-                    pack_ref[pl.ds(base + 8 + 2 * g + h, 1), :] = gather_blocks(some)[:1]
-        lane = iota(1)
-        speeds = jnp.zeros((8, 128), f32)
-        for k in range(4 * STEPS):
-            speeds = jnp.where(lane == k, flow_ref[(k // 4 * L + level) * 4 + k % 4], speeds)
-        pack_ref[pl.ds(3 * LINES, 1), :] = speeds[:1]
-        pack_ref[pl.ds(3 * LINES + 1, EXTRA - 3 * LINES - 1), :] = jnp.zeros(
-            (EXTRA - 3 * LINES - 1, 128), f32
-        )
-        for member in range(members):
-            for k in range(EXTRA // 8):
-                out_ref[member, pl.ds(FRAME + 8 * k, 8), :] = pack_ref[pl.ds(8 * k, 8), :]
+    lax.fori_loop(0, members, one, 0, unroll=8)
+    row = lax.axis_index("member")
+    variable, level = row // L, row % L
+    for c in range(ROWS):
+        line = pl.ds(L * c + level, 1)
+        rows_ref[0, pl.ds(c, 1), :] = rate_ref[pl.ds(c, 1), :]
+        rows_ref[1, pl.ds(c, 1), :] = weight_ref[variable, line, :]
+        rows_ref[2, pl.ds(c, 1), :] = target_ref[variable, line, :]
+
+    def spread(kind, c):
+        return spread_row(rows_ref[kind, pl.ds(c, 1), :])
+
+    for place, c in enumerate((0, 1, 2, 3, 28, 29, 30, 31)):
+        pack_ref[pl.ds(place, 1), :] = rows_ref[0, pl.ds(c, 1), :]
+    for g in range(3):
+        for h in range(2):
+            some = [spread(0, 2 * (2 + 4 * g + j) + h) for j in range(4)]
+            pack_ref[pl.ds(8 + 2 * g + h, 1), :] = gather_blocks(some)[:1]
+    for kind in range(1, 3):
+        base = LINES + (kind - 1) * SHALLOW
+        pack_ref[pl.ds(base, 1), :] = rows_ref[kind, pl.ds(0, 1), :]
+        pack_ref[pl.ds(base + 1, 1), :] = rows_ref[kind, pl.ds(ROWS - 1, 1), :]
+        for half in range(2):
+            some = [spread(kind, 16 * half + j) for j in range(16)]
+            pack_ref[pl.ds(base + 2 + half, 1), :] = gather_corners(some)[:1]
+    lane = iota(1)
+    speeds = jnp.zeros((8, 128), f32)
+    for k in range(4 * STEPS):
+        speeds = jnp.where(lane == k, flow_ref[k // 4, level, k % 4], speeds)
+    base = LINES + 2 * SHALLOW
+    pack_ref[pl.ds(base, 1), :] = speeds[:1]
+    pack_ref[pl.ds(base + 1, EXTRA - base - 1), :] = jnp.zeros((EXTRA - base - 1, 128), f32)
+    for member in range(members):
+        for k in range(EXTRA // 8):
+            out_ref[member, pl.ds(FRAME + 8 * k, 8), :] = pack_ref[pl.ds(8 * k, 8), :]
+
+
+def increment_kernel(spread_ref, smoothed_ref, out_ref, total_ref):
+    step = pl.program_id(0)
+
+    @pl.when(step == 0)
+    def _():
+        total_ref[...] = jnp.zeros(total_ref.shape, f32)
+
+    for k in range(FIELD // 8):
+        line = pl.ds(8 * k, 8)
+        fields = [smoothed_ref[m, line, :] for m in range(GROUP)]
+        for v in range(V):
+            terms = [spread_ref[m, v, line, :] * fields[m] for m in range(GROUP)]
+            while len(terms) > 1:
+                terms = [a + b for a, b in zip(terms[0::2], terms[1::2])]
+            total_ref[v, line, :] = total_ref[v, line, :] + terms[0]
+
+    @pl.when(step == pl.num_programs(0) - 1)
+    def _():
+        for v in range(V):
+            for c in range(ROWS):
+                out_ref[pl.ds(L * v, L), c, :] = total_ref[v, pl.ds(L * c, L), :]
+
+
+def project_kernel(spread_ref, rows_ref, out_ref, frame_ref, lines_ref):
+    @pl.when(pl.program_id(0) == 0)
+    def _():
+        for v in range(V):
+            for c in range(ROWS):
+                lines_ref[v, pl.ds(L * c, L), :] = rows_ref[pl.ds(L * v, L), c, :]
+
+    for k in range(FIELD // 8):
+        line = pl.ds(8 * k, 8)
+        fields = [lines_ref[v, line, :] for v in range(V)]
+        for m in range(GROUP):
+            terms = [spread_ref[m, v, line, :] * fields[v] for v in range(V)]
+            value = (terms[0] + terms[1]) + (terms[2] + terms[3])
+            out_ref[m, line, :] = value
+    for m in range(GROUP):
+        pack_frame([out_ref[m, pl.ds(8 * k, 8), :] for k in range(FIELD // 8)], frame_ref, m)
 
 
 def set_ghosts(ends, sides, first, last, seam_ref, side_ref):
@@ -320,7 +371,7 @@
         mirror = 7 - iota(0)
         found = []
         for k in range(2):
-            index, kind, flip = table_ref[k, 0], table_ref[k, 1], table_ref[k, 2]
+            index, kind, flip = [spread_row(table_ref[pl.ds(3 * k + i, 1), :]) for i in range(3)]
             got = [jnp.where(kind != 0, pick(sides[q], index), pick(ends[q], index)) for q in range(8)]
             back = [
                 jnp.take_along_axis(got[7 - q], mirror, axis=0, mode="promise_in_bounds")
@@ -349,11 +400,12 @@
         for group in range(2):
             tiles = pl.ds(8 * group, 8)
             for kind in range(2):
-                start = FRAME + LINES + kind * LINES
-                cells = split_halves(unpack([x_ref[tiles, start + i, :] for i in range(LINES)]))
+                start = FRAME + LINES + kind * SHALLOW
+                lines = [x_ref[tiles, start + i, :] for i in range(SHALLOW)]
+                cells = split_halves(unpack_shallow(lines))
                 for r in range(ROWS):
                     target_ref[kind, group, r] = cells[r]
-            speeds = x_ref[tiles, FRAME + 3 * LINES, :]
+            speeds = x_ref[tiles, FRAME + LINES + 2 * SHALLOW, :]
             for k in range(4 * STEPS):
                 speed_ref[group, k] = jnp.broadcast_to(speeds[:, k : k + 1], (8, 128))
 
@@ -415,6 +467,7 @@
                 out_ref[2 * pair + 1, line, :] = b
 
 
+GRANT = pltpu.CompilerParams(vmem_limit_bytes=16 * 1024 * 1024)
 VMEM = pl.BlockSpec(memory_space=pltpu.VMEM)
 SMEM = pl.BlockSpec(memory_space=pltpu.SMEM)
 
@@ -423,25 +476,50 @@
     return jax.ShapeDtypeStruct(dims, f32)
 
 
-def pack_first(lines, own, flow, rate, weight, target):
+def pack_first(lines, flow, rate, weight, target):
     return pl.pallas_call(
         pack_kernel,
         out_shape=(shape(lines.shape[0], FRAME + EXTRA, 128), shape(3, ROWS, 128)),
-        in_specs=[VMEM, SMEM, SMEM, VMEM, VMEM, VMEM],
+        in_specs=[VMEM, SMEM, VMEM, VMEM, VMEM],
         out_specs=(VMEM, VMEM),
         scratch_shapes=[pltpu.VMEM((EXTRA, 128), f32)],
         name="pack_first",
-    )(lines, own, flow, rate, weight, target)
-
-
-def pack(lines):
+    )(lines, flow, rate, weight, target)
+
+
+def members_block(*dims):
+    return pl.BlockSpec((GROUP, *dims), lambda i: (i,) + (0,) * len(dims))
+
+
+def whole_block(*dims):
+    return pl.BlockSpec(dims, lambda i: (0,) * len(dims))
+
+
+def increments(spread, smoothed):
     return pl.pallas_call(
-        pack_kernel,
-        out_shape=shape(lines.shape[0], FRAME, 128),
-        in_specs=[VMEM],
-        out_specs=VMEM,
-        name="pack",
-    )(lines)
+        increment_kernel,
+        grid=(spread.shape[0] // GROUP,),
+        out_shape=shape(V * L, ROWS, 128),
+        in_specs=[members_block(V, FIELD, 128), members_block(FIELD, 128)],
+        out_specs=whole_block(V * L, ROWS, 128),
+        scratch_shapes=[pltpu.VMEM((V, FIELD, 128), f32)],
+        compiler_params=GRANT,
+        name="increments",
+    )(spread, smoothed)
+
+
+def project(spread, rows):
+    members = spread.shape[0]
+    return pl.pallas_call(
+        project_kernel,
+        grid=(members // GROUP,),
+        out_shape=(shape(members, FIELD, 128), shape(members, FRAME, 128)),
+        in_specs=[members_block(V, FIELD, 128), whole_block(V * L, ROWS, 128)],
+        out_specs=(members_block(FIELD, 128), members_block(FRAME, 128)),
+        scratch_shapes=[pltpu.VMEM((V, FIELD, 128), f32)],
+        compiler_params=GRANT,
+        name="project",
+    )(spread, rows)
 
 
 FIELDS = pltpu.VMEM((ROWS, S, 128), f32)
@@ -460,6 +538,7 @@
         in_specs=[VMEM, VMEM],
         out_specs=(VMEM, VMEM, VMEM, VMEM),
         scratch_shapes=FRAME_SCRATCH,
+        compiler_params=GRANT,
         name="frame_forward",
     )(table, received)
 
@@ -471,6 +550,7 @@
         in_specs=[VMEM, VMEM, VMEM],
         out_specs=VMEM,
         scratch_shapes=FRAME_SCRATCH + [FIELDS],
+        compiler_params=GRANT,
         name="frame_adjoint",
     )(table, received, rate)
 
@@ -482,6 +562,7 @@
         in_specs=[VMEM],
         out_specs=VMEM,
         cost_estimate=pl.CostEstimate(flops=2_000_000, bytes_accessed=1_100_000, transcendentals=0),
+        compiler_params=GRANT,
         name="spread_rate",
     )(rows)
 
@@ -493,13 +574,13 @@
         in_specs=[VMEM] * (3 + len(added)),
         out_specs=VMEM,
         scratch_shapes=FRAME_SCRATCH + [FIELDS] * adjoint,
+        compiler_params=GRANT,
         name="tile_adjoint" if adjoint else "tile_forward",
     )(lines, series, rate, *added)
 
 
 def transport_kernel(
     src_ref,
-    own_ref,
     flip_ref,
     x_ref,
     target_ref,
@@ -542,11 +623,11 @@
                 ghosts = [ghosts[d] * c[d] for d in range(4)]
             else:
                 c = [c[1], c[0], c[3], c[2]]
-            flips = [flip_ref[tiles[d], :] for d in range(4)]
+            flips = [jnp.broadcast_to(flip_ref[tiles[d], :], (8, 128)) for d in range(4)]
             top, bottom, sides = placed_ghosts(ghosts, flips)
             first = field_ref[group, 0]
             last = field_ref[group, ROWS - 1]
-            owned = iota(0) + 8 * group == own_ref[0]
+            owned = iota(0) + 8 * group == lax.axis_index("tile")
             previous = None
             here = first
             for r in range(ROWS):
@@ -586,16 +667,16 @@
         cells = join_halves([field_ref[group, r] for r in range(ROWS)])
         for c in range(ROWS):
             plain_ref[pl.ds(8 * group, 8), c, :] = cells[c]
-    mine = plain_ref[own_ref[0]]
+    mine = plain_ref[lax.axis_index("tile")]
     for other in range(out_ref.shape[0]):
         out_ref[other] = mine
 
 
-def transport(src, own, flip, gathered, target, speed, rows, copies):
+def transport(src, flip, gathered, target, speed, rows, copies):
     return pl.pallas_call(
         transport_kernel,
         out_shape=shape(copies, ROWS, 128),
-        in_specs=[SMEM, SMEM] + [VMEM] * 5,
+        in_specs=[SMEM] + [VMEM] * 5,
         out_specs=VMEM,
         scratch_shapes=[
             pltpu.VMEM((2, ROWS, 8, 128), f32),
@@ -604,8 +685,9 @@
             pltpu.VMEM((TILES, ROWS, 128), f32),
             pltpu.VMEM((2, ROWS, 8, 128), f32),
         ],
+        compiler_params=GRANT,
         name="transport",
-    )(src, own, flip, gathered, target, speed, rows)
+    )(src, flip, gathered, target, speed, rows)
 
 
 def exchange(values, axis):
@@ -643,17 +725,13 @@
 
     place = (neighbour_edge % 2) * S + neighbour_tile * L
     index = by_lane(place) + jnp.arange(128, dtype=jnp.int32) % L
-    table = jnp.stack([index, by_lane(neighbour_edge // 2), by_lane(flips)], axis=1)
-    table = jnp.broadcast_to(table[:, :, None], (2, 3, 8, 128))
-    flip = jnp.broadcast_to(flips.T.reshape(4 * TILES, 1), (4 * TILES, 128))
-    own = lax.axis_index("tile").reshape(1)
-    row = lax.axis_index("member")
+    table = jnp.stack([index, by_lane(neighbour_edge // 2), by_lane(flips)], axis=1).reshape(6, 128)
+    flip = flips.T.reshape(4 * TILES, 1)
     control_lines = to_lines(control[:, 0])
 
     packed, rows = pack_first(
         control_lines,
-        jnp.stack([row // L, row % L]),
-        flow.reshape(-1),
+        flow[:, 0],
         diffusivity.reshape(ROWS, 128),
         to_lines(obs_weight[0]),
         to_lines(observed[0]),
@@ -664,16 +742,12 @@
     smoothed = tile_smooth(False, control_lines, exchange(series, "tile"), own_rate)
 
     spread = to_lines(perturbations[:, 0])
-    partial = jnp.sum(spread * smoothed[:, None], axis=0)
-    partial = jnp.swapaxes(partial.reshape(V, ROWS, L, 128), 1, 2).reshape(V * L, ROWS, 128)
-    increment = jnp.sum(exchange(partial, "member"), axis=0)
+    increment = jnp.sum(exchange(increments(spread, smoothed), "member"), axis=0)
     gathered = exchange(jnp.broadcast_to(increment[None], (TILES, ROWS, 128)), "tile")
-    sensitivity = transport(source, own, flip, gathered, goal, speed, rows, V * L)
+    sensitivity = transport(source, flip, gathered, goal, speed, rows, V * L)
     sensitivity = exchange(sensitivity, "member")
-    sensitivity = jnp.swapaxes(sensitivity.reshape(V, L, ROWS, 128), 1, 2).reshape(V, FIELD, 128)
-
-    projected = jnp.sum(spread * sensitivity[None], axis=1)
-    series = frame_adjoint(table, exchange(pack(projected), "tile"), rate)
+    projected, frames = project(spread, sensitivity)
+    series = frame_adjoint(table, exchange(frames, "tile"), rate)
     mixed = tile_smooth(True, projected, exchange(series, "tile"), own_rate, control_lines)
     return from_lines(mixed)[:, None]
 

time: 194 us -> 170 us (0.88)
  Pallas kernels: 40.3 us -> 28.4 us
  other arithmetic: 7.88 us -> 2.09 us
  blocking collectives: 69.3 us -> 65 us
    unnamed x6 -> x26, local copies, waits for them, and re-layouts: 1.09 us -> 8.65 us
    another operation x1 -> x0, local copies, waits for them, and re-layouts: 6.07 us -> none  [to_lines(): fields = fields.reshape(*lead, L, ROWS, 128)]
    reduce_sum x3 -> x1, other arithmetic: 5.79 us -> 0.02 us  [body(): jnp.sum(exchange(increments(spread, smoothed), 'member'), axis=0)]
    pallas_call x2, Pallas kernels: 14.2 us -> 9.48 us  [tile_smooth(): pl.pallas_call(functools.partial(tile_kernel, adjoint), out_shape=shape(l...]
    all_to_all x4, blocking collectives: 69.3 us -> 65 us  [exchange(): return lax.all_to_all(values, axis, split_axis=0, concat_axis=0, tiled=True)]
    pallas_call x1, Pallas kernels: 6.85 us -> 4.65 us  [frame_adjoint(): pl.pallas_call(functools.partial(frame_kernel, True), out_shape=shape(TIL...]
  transfers between devices with their start and end apart: 3 -> 3, of which waited for: 3 -> 3; matrix products, arithmetic and copies ran while one was open for 5% -> 4% of each run, Pallas kernels for 1% -> 0%
where the time goes in v3:
time: 170 us; the launch traced here: 169 us
  blocking collectives  65 us (38%)
  waiting for transfers between devices  42.9 us (25%)
  Pallas kernels  28.4 us (17%)
  starting transfers between devices  16.7 us (10%)
  local copies, waits for them, and re-layouts  13.7 us (8%)
  other arithmetic  2.09 us (1%)
    all_to_all x4, blocking collectives, exchange(): return lax.all_to_all(values, axis, split_axis=0, concat_axis=0, tiled=True)  65 us
    all_to_all x3, waiting for transfers between devices, exchange(): return lax.all_to_all(values, axis, split_axis=0, concat_axis=0, tiled=True)  42.9 us
    all_to_all x3, starting transfers between devices, exchange(): return lax.all_to_all(values, axis, split_axis=0, concat_axis=0, tiled=True)  16.7 us
    pallas_call x2, Pallas kernels, tile_smooth(): pl.pallas_call(functools.partial(tile_kernel, adjoint), out_shape=shape(l...  9.48 us
    unnamed x26, local copies, waits for them, and re-layouts  8.65 us
    pallas_call x1, Pallas kernels, frame_forward(): pl.pallas_call(functools.partial(frame_kernel, False), out_shape=(shape(T...  5.74 us
    pallas_call x1, Pallas kernels, frame_adjoint(): pl.pallas_call(functools.partial(frame_kernel, True), out_shape=shape(TIL...  4.65 us
    pallas_call x1, Pallas kernels, transport(): pl.pallas_call(transport_kernel, out_shape=shape(copies, ROWS, 128), in_s...  4 us
  transfers between devices with their start and end apart: 3, of which 3 were waited for; matrix products, arithmetic and copies ran while one was open for 4% of the time, Pallas kernels for 0%

profile of v3, /device:TPU:2, one launch (start us, length us, event | category | flops | bytes accessed | tf_op | source)
XLA Modules:
  0.0 169.0 jit_solution(3972819006579375803)
XLA Ops:
  0.0 2.7 %pack_first.1 = (f32[16,80,128]{2,1,0:T(8,128)}, f32[3,32,128]{2,1,0:T(8,128)}) custom-call(f32[16,128,128]{2,1,0:T(8,128)} %bitcast.36, f32[2,4,4]{2,1,0:T(4,128)} %bitcast.44, f32[32,128]{1,0:T(8,128)} %bitcast.43, f32[4,128,128]{2,1,0:T(8,128)} %bitcast.39, f32[4,128,128]{2,1,0:T(8,128)} %bitcast.40), custom_call_target="tpu_custom_call" | custom-call | tf_op jit(solution)/shard_map/pack_first/pallas_call | solution.py:480
  2.8 9.6 %all-to-all-start = ((f32[16,80,128]{2,1,0:T(8,128)}), f32[16,80,128]{2,1,0:T(8,128)S(1)}, u32[]{:S(2)}, u32[]{:S(2)}) async-start(f32[16,80,128]{2,1,0:T(8,128)} %get-tuple-element.13), calls=%async_computation | async-start | bytes 1310720 | tf_op jit(solution)/shard_map/all_to_all | solution.py:694
  12.3 1.3 fusion.3
  13.6 0.1 reshape.86
  13.7 0.1 broadcast_in_dim.16
  13.8 0.1 reshape.87
  13.9 0.1 reshape.88
  14.0 0.1 broadcast_in_dim.17
  14.1 0.1 stack_reshape.6
  14.2 0.8 fusion
  14.9 0.1 copy.20
  15.0 0.1 reshape.89
  15.1 0.1 broadcast_in_dim.18
  15.2 0.1 stack_reshape.7
  15.4 0.0 copy-start.9
  15.4 17.3 %all-to-all-done.x_ref = f32[16,80,128]{2,1,0:T(8,128)S(1)} async-done(((f32[16,80,128]{2,1,0:T(8,128)}), f32[16,80,128]{2,1,0:T(8,128)S(1)}, u32[]{:S(2)}, u32[]{:S(2)}) %all-to-all-start) | async-done | bytes 655392 | tf_op jit(solution)/shard_map/all_to_all | solution.py:694
  32.7 5.7 %frame_forward.1 = (f32[16,64,128]{2,1,0:T(8,128)}, f32[32,64,128]{2,1,0:T(8,128)S(1)}, f32[2,2,32,8,128]{4,3,2,1,0:T(8,128)S(1)}, f32[2,8,8,128]{3,2,1,0:T(8,128)S(1)}) custom-call(s32[6,128]{1,0:T(8,128)S(1)} %reshape.90.table_ref, f32[16,80,128]{2,1,0:T(8,128)S(1)} %all-to-all-done.x_ref), custom_call_target="tpu_custom_call" | custom-call | tf_op jit(solution)/shard_map/frame_forward/pallas_call | solution.py:530
  38.5 1.0 copy-done.3
  39.4 0.8 copy-done.5
  40.2 3.6 %all-to-all-start.1 = ((f32[16,64,128]{2,1,0:T(8,128)}), f32[16,64,128]{2,1,0:T(8,128)S(1)}, u32[]{:S(2)}, u32[]{:S(2)}) async-start(f32[16,64,128]{2,1,0:T(8,128)} %get-tuple-element.14), calls=%async_computation.1 | async-start | bytes 1048576 | tf_op jit(solution)/shard_map/all_to_all | solution.py:694
  43.8 0.0 copy-done.12
  43.8 0.0 copy-done.9
  43.8 0.0 copy-start.7
  43.8 0.8 copy-done.7
  44.6 0.3 spread_rate.1.rate_ref
  44.9 15.4 %all-to-all-done.1.series_ref = f32[16,64,128]{2,1,0:T(8,128)S(1)} async-done(((f32[16,64,128]{2,1,0:T(8,128)}), f32[16,64,128]{2,1,0:T(8,128)S(1)}, u32[]{:S(2)}, u32[]{:S(2)}) %all-to-all-start.1) | async-done | bytes 524320 | tf_op jit(solution)/shard_map/all_to_all | solution.py:694
  60.3 4.1 %tile_forward.1.smoothed_ref = f32[16,128,128]{2,1,0:T(8,128)S(1)} custom-call(f32[16,128,128]{2,1,0:T(8,128)S(1)} %bitcast.37, f32[16,64,128]{2,1,0:T(8,128)S(1)} %all-to-all-done.1.series_ref, f32[32,64,128]{2,1,0:T(8,128)S(1)} %spread_rate.1.rate_ref), custom_call_target="tpu_custom_call" | custom-call | tf_op jit(solution)/shard_map/tile_forward/pallas_call | solution.py:571
  64.5 0.0 copy-start
  64.5 2.2 %copy-done = f32[16,1,4,4,4096]{4,3,2,1,0:T(4,128)S(1)} copy-done((f32[16,1,4,4,4096]{4,3,2,1,0:T(4,128)S(1)}, f32[16,1,4,4,4096]{4,3,2,1,0:T(4,128)}, u32[]{:S(2)}) %copy-start) | copy-done | bytes 4194328
  66.6 0.6 increments.1
  67.2 14.0 %all_to_all.35 = f32[16,32,128]{2,1,0:T(8,128)S(1)} all-to-all(f32[16,32,128]{2,1,0:T(8,128)S(1)} %increments.1), channel_id=1, replica_groups=mesh['member'=16,'tile'=16] {'member'}, dimensions={0} | all-to-all | bytes 524288 | tf_op jit(solution)/shard_map/all_to_all | solution.py:694
  81.2 0.7 broadcast_in_dim.19
  81.9 3.5 %all-to-all-start.3 = ((f32[16,32,128]{2,1,0:T(8,128)}), f32[16,32,128]{2,1,0:T(8,128)S(1)}, u32[]{:S(2)}, u32[]{:S(2)}) async-start(f32[16,32,128]{2,1,0:T(8,128)} %broadcast_in_dim.19), calls=%async_computation.3 | async-start | bytes 524288 | tf_op jit(solution)/shard_map/all_to_all | solution.py:694
  85.5 0.8 reshape.95.flip_ref
  86.2 1.3 copy.19
  87.6 1.4 reshape.83.src_ref
  88.9 10.2 %all-to-all-done.3.x_ref = f32[16,32,128]{2,1,0:T(8,128)S(1)} async-done(((f32[16,32,128]{2,1,0:T(8,128)}), f32[16,32,128]{2,1,0:T(8,128)S(1)}, u32[]{:S(2)}, u32[]{:S(2)}) %all-to-all-start.3) | async-done | bytes 262176 | tf_op jit(solution)/shard_map/all_to_all | solution.py:694
  99.1 1.0 copy-done.6
  100.2 0.7 copy-done.11
  100.8 4.0 %transport.1 = f32[16,32,128]{2,1,0:T(8,128)S(1)} custom-call(s32[64]{0:T(128)S(1)} %copy-done.11, s32[64,1]{1,0:T(8,128)S(1)} %reshape.95.flip_ref, f32[16,32,128]{2,1,0:T(8,128)S(1)} %all-to-all-done.3.x_ref, f32[2,2,32,8,128]{4,3,2,1,0:T(8,128)S(1)} %copy-done.6, f32[2,8,8,128]{3,2,1,0:T(8,128)S(1)} %get-tuple-element.17.speed_ref, ...), custom_call_target="tpu_custom_call" | custom-call | tf_op jit(solution)/shard_map/transport/pallas_call | solution.py:676
  104.8 11.2 %all_to_all.36.rows_ref = f32[16,32,128]{2,1,0:T(8,128)S(1)} all-to-all(f32[16,32,128]{2,1,0:T(8,128)S(1)} %transport.1), channel_id=1, replica_groups=mesh['member'=16,'tile'=16] {'member'}, dimensions={0} | all-to-all | bytes 524288 | tf_op jit(solution)/shard_map/all_to_all | solution.py:694
  116.1 2.2 %copy-done.1 = f32[16,1,4,4,4096]{4,3,2,1,0:T(4,128)S(1)} copy-done((f32[16,1,4,4,4096]{4,3,2,1,0:T(4,128)S(1)}, f32[16,1,4,4,4096]{4,3,2,1,0:T(4,128)}, u32[]{:S(2)}) %copy-start.1) | copy-done | bytes 4194328
  118.3 0.8 project.1
  119.1 20.2 %all_to_all.37.x_ref = f32[16,56,128]{2,1,0:T(8,128)S(1)} all-to-all(f32[16,56,128]{2,1,0:T(8,128)S(1)} %get-tuple-element.19), channel_id=1, replica_groups=mesh['member'=16,'tile'=16] {'tile'}, dimensions={0} | all-to-all | bytes 917504 | tf_op jit(solution)/shard_map/all_to_all | solution.py:694
  139.4 0.0 copy-done.10
  139.4 4.7 %frame_adjoint.1 = f32[16,64,128]{2,1,0:T(8,128)S(1)} custom-call(s32[6,128]{1,0:T(8,128)S(1)} %copy-done.10, f32[16,56,128]{2,1,0:T(8,128)S(1)} %all_to_all.37.x_ref, f32[32,64,128]{2,1,0:T(8,128)S(1)} %copy-done.4), custom_call_target="tpu_custom_call" | custom-call | tf_op jit(solution)/shard_map/frame_adjoint/pallas_call | solution.py:547
  144.0 19.6 %all_to_all.38.series_ref = f32[16,64,128]{2,1,0:T(8,128)S(1)} all-to-all(f32[16,64,128]{2,1,0:T(8,128)S(1)} %frame_adjoint.1), channel_id=1, replica_groups=mesh['member'=16,'tile'=16] {'tile'}, dimensions={0} | all-to-all | bytes 1048576 | tf_op jit(solution)/shard_map/all_to_all | solution.py:694
  163.6 5.4 %tile_adjoint.1 = f32[16,128,128]{2,1,0:T(8,128)} custom-call(f32[16,128,128]{2,1,0:T(8,128)S(1)} %get-tuple-element.18.x_ref, f32[16,64,128]{2,1,0:T(8,128)S(1)} %all_to_all.38.series_ref, f32[32,64,128]{2,1,0:T(8,128)S(1)} %spread_rate.1.rate_ref, f32[16,128,128]{2,1,0:T(8,128)S(1)} %bitcast.38), custom_call_target="tpu_custom_call" | custom-call | tf_op jit(solution)/shard_map/tile_adjoint/pallas_call | solution.py:571
  (19 shorter events, 0.1 us)
Async XLA Ops:
  0.0 60.3 %copy-start.2 = (f32[16,1,4,4096]{3,2,1,0:T(4,128)S(1)}, f32[16,1,4,4096]{3,2,1,0:T(4,128)}, u32[]{:S(2)}) copy-start(f32[16,1,4,4096]{3,2,1,0:T(4,128)} %param.9) | copy-start | bytes 3145732
  2.8 30.0 %all-to-all-start = ((f32[16,80,128]{2,1,0:T(8,128)}), f32[16,80,128]{2,1,0:T(8,128)S(1)}, u32[]{:S(2)}, u32[]{:S(2)}) async-start(f32[16,80,128]{2,1,0:T(8,128)} %get-tuple-element.13), calls=%async_computation | async-start | bytes 1310720 | tf_op jit(solution)/shard_map/all_to_all | solution.py:694
  15.0 28.8 %copy-start.12 = (s32[16,4,1]{0,1,2:T(4,128)}, s32[16,4,1]{0,1,2:T(4,128)S(1)}, u32[]{:S(2)}) copy-start(s32[16,4,1]{0,1,2:T(4,128)S(1)} %copy.20) | copy-start | bytes 772
  15.4 28.4 %copy-start.9 = (s32[6,128]{1,0:T(8,128)}, s32[6,128]{1,0:T(8,128)S(1)}, u32[]{:S(2)}) copy-start(s32[6,128]{1,0:T(8,128)S(1)} %reshape.90.table_ref) | copy-start | bytes 9220
  38.5 1.0 copy-start.3
  39.4 0.8 copy-start.5
  40.2 20.1 %all-to-all-start.1 = ((f32[16,64,128]{2,1,0:T(8,128)}), f32[16,64,128]{2,1,0:T(8,128)S(1)}, u32[]{:S(2)}, u32[]{:S(2)}) async-start(f32[16,64,128]{2,1,0:T(8,128)} %get-tuple-element.14), calls=%async_computation.1 | async-start | bytes 1048576 | tf_op jit(solution)/shard_map/all_to_all | solution.py:694
  43.8 0.8 copy-start.7
  64.5 2.2 %copy-start = (f32[16,1,4,4,4096]{4,3,2,1,0:T(4,128)S(1)}, f32[16,1,4,4,4096]{4,3,2,1,0:T(4,128)}, u32[]{:S(2)}) copy-start(f32[16,1,4,4,4096]{4,3,2,1,0:T(4,128)} %param.10) | copy-start | bytes 12582916
  66.6 32.5 %copy-start.8 = (f32[3,32,128]{2,1,0:T(8,128)S(1)}, f32[3,32,128]{2,1,0:T(8,128)}, u32[]{:S(2)}) copy-start(f32[3,32,128]{2,1,0:T(8,128)} %get-tuple-element.15.rows_ref) | copy-start | bytes 147460
  81.2 58.2 %copy-start.4 = (f32[32,64,128]{2,1,0:T(8,128)S(1)}, f32[32,64,128]{2,1,0:T(8,128)}, u32[]{:S(2)}) copy-start(f32[32,64,128]{2,1,0:T(8,128)} %copy-done.3) | copy-start | bytes 3145732
  81.9 17.2 %all-to-all-start.3 = ((f32[16,32,128]{2,1,0:T(8,128)}), f32[16,32,128]{2,1,0:T(8,128)S(1)}, u32[]{:S(2)}, u32[]{:S(2)}) async-start(f32[16,32,128]{2,1,0:T(8,128)} %broadcast_in_dim.19), calls=%async_computation.3 | async-start | bytes 524288 | tf_op jit(solution)/shard_map/all_to_all | solution.py:694
  99.1 1.0 copy-start.6
  100.2 0.7 copy-start.11
  100.8 38.5 %copy-start.10 = (s32[6,128]{1,0:T(8,128)S(1)}, s32[6,128]{1,0:T(8,128)}, u32[]{:S(2)}) copy-start(s32[6,128]{1,0:T(8,128)} %copy-done.9) | copy-start | bytes 9220
  116.1 2.2 %copy-start.1 = (f32[16,1,4,4,4096]{4,3,2,1,0:T(4,128)S(1)}, f32[16,1,4,4,4096]{4,3,2,1,0:T(4,128)}, u32[]{:S(2)}) copy-start(f32[16,1,4,4,4096]{4,3,2,1,0:T(4,128)} %param.10) | copy-start | bytes 12582916
